TPU v7x, 32 devices: a whole 2x2x4 slice. The times are simulated.
32 devices in a mesh: row: 4 (over z), col: 8 (over y, x, core).
Axes of the slice: x: 2, y: 2, z: 4, core: 2. Of those that a mesh axis runs over, the one named last changes fastest.
Arguments:
- hessian: float32 [18432, 18432], P('row', 'col'), may hold values from -1 to 5, as said below
- right_side: float32 [18432, 512], P('row'), may hold values from -6 to 6
- mask: int32 [18432, 512], P('row'), may hold values 0 or 1
- damping: float32 [1], replicated, may hold values from 0.4 to 1.2
Outputs:
- solution: float32 [18432, 512], P('row')
Inputs may be any that keep to these rules, and one draw needn't show every extreme that they name: hessian is symmetric and positive definite.
All inputs are finite; a program needn't handle non-finite values. No bound on the sum of `mask` on one device may be relied on, other than what follows from the above.
Results may differ from a plain program's by a relative error of at most 0.0001.
Values sent between devices are 32-bit elements; how exact they have to be, the bound alone decides.
No kernel may reach another device: no remote copies, remote signals or barrier semaphores. Data moves between devices by JAX's collectives and lax.ppermute only.
A program may use at most 192 MiB of HBM per device.

v0:
```python
import functools

import jax
import jax.numpy as jnp
from jax import lax
from jax.experimental import pallas as pl
from jax.experimental.pallas import tpu as pltpu
from jax.sharding import PartitionSpec as P


CHUNKS = 2
epsilon = 1e-06
F32, BF16 = jnp.float32, jnp.bfloat16
VMEM_LIMIT = 48 << 20


def strip_of(size):
    return next(s for s in (64, 48, 32, 16) if size % s == 0)


def split(value):
    high = value.astype(BF16)
    return high, (value - high.astype(F32)).astype(BF16)


def down(left, right):
    return lax.dot_general(
        left, right, (((0,), (0,)), ((), ())), preferred_element_type=F32
    )


def copy_strips(source, source_base, target, target_base, size):
    strip = strip_of(size)

    def body(s, carry):
        here = pl.ds(pl.multiple_of(source_base + s * strip, 16), strip)
        there = pl.ds(pl.multiple_of(target_base + s * strip, 16), strip)
        target[there, :] = source[here, :]
        return carry

    lax.fori_loop(0, size // strip, body, 0)


def product_kernel(layout, place_ref, h_ref, *refs):
    n_piece, ratio, piece, sub, low_terms, fresh, n_after = layout
    n_in = 2 if fresh else ratio
    inputs, refs = refs[:n_in], refs[n_in + n_after :]
    outputs = refs[:n_piece]
    x_out = None if fresh else refs[n_piece]
    terms, sums = refs[-2], refs[-1]
    step = pl.program_id(0)
    rows, width = h_ref.shape
    columns = sums.shape[1]
    block = n_piece * piece
    strip = strip_of(piece)

    def keep(value, at):
        high, low = split(value)
        terms[at, :columns] = high
        if low_terms:
            terms[at, columns:] = low

    @pl.when(step == 0)
    def _():
        if fresh:
            right_ref, mask_ref = inputs

            def body(s, carry):
                at = pl.ds(pl.multiple_of(s * strip, strip), strip)
                keep(mask_ref[at, :].astype(F32) * right_ref[at, :], at)
                return carry

            lax.fori_loop(0, rows // strip, body, 0)
        else:
            for j in range(ratio):
                for k in range(n_piece):
                    base = (place_ref[1] ^ j) * block + (place_ref[0] ^ k) * piece

                    def body(s, carry, j=j, k=k, base=base):
                        start = pl.multiple_of(k * piece + s * strip, strip)
                        at = pl.ds(pl.multiple_of(base + s * strip, 16), strip)
                        value = inputs[j][pl.ds(start, strip), :]
                        keep(value, at)
                        x_out[at, :] = value
                        return carry

                    lax.fori_loop(0, piece // strip, body, 0)

    summed = None
    for s in range(rows // sub):
        at = slice(s * sub, (s + 1) * sub)
        high, low = split(h_ref[at, :])
        part = down(high, terms[at, :])
        if low_terms:
            part = part[:, :columns] + part[:, columns:]
        part = part + down(low, terms[at, :columns])
        summed = part if summed is None else summed + part
    sums[pl.ds(pl.multiple_of(step * width, 128), width), :] = summed

    @pl.when(step == pl.num_programs(0) - 1)
    def _():
        for k in range(n_piece):
            copy_strips(sums, (place_ref[0] ^ k) * piece, outputs[k], 0, piece)


def product(hessian, place, inputs, columns, piece, chunk=None, after=()):
    low_terms = True
    rows, block = hessian.shape
    n_piece = block // piece
    ratio = rows // block
    fresh = chunk is not None
    width = max(w for w in (128, 256, 384) if block % w == 0 and w * rows <= 1 << 21)
    sub = min(rows, 2304)
    if rows % sub:
        sub = rows
    whole = lambda shape, at=0: pl.BlockSpec(shape, lambda i, p: (0, at))
    if fresh:
        in_specs = [whole((rows, columns), chunk)] * 2
    else:
        in_specs = [whole((block, columns))] * ratio
    out_shape = [jax.ShapeDtypeStruct((piece, columns), F32)] * n_piece
    out_specs = [whole((piece, columns))] * n_piece
    if not fresh:
        out_shape.append(jax.ShapeDtypeStruct((rows, columns), F32))
        out_specs.append(whole((rows, columns)))
    in_specs += [pl.BlockSpec(memory_space=pl.ANY)] * len(after)
    layout = (n_piece, ratio, piece, sub, low_terms, fresh, len(after))
    passes = 3 if low_terms else 2
    return pl.pallas_call(
        functools.partial(product_kernel, layout),
        out_shape=out_shape,
        grid_spec=pltpu.PrefetchScalarGridSpec(
            num_scalar_prefetch=1,
            grid=(block // width,),
            in_specs=[pl.BlockSpec((rows, width), lambda i, p: (0, i))] + in_specs,
            out_specs=out_specs,
            scratch_shapes=[
                pltpu.VMEM((rows, columns * (2 if low_terms else 1)), BF16),
                pltpu.VMEM((block, columns), F32),
            ],
        ),
        compiler_params=pltpu.CompilerParams(
            dimension_semantics=("arbitrary",), vmem_limit_bytes=VMEM_LIMIT
        ),
        cost_estimate=pl.CostEstimate(
            flops=2 * passes * rows * block * columns,
            bytes_accessed=4 * (rows * block + rows * columns + block * columns),
            transcendentals=0,
        ),
    )(place, hessian, *inputs, *after)


def assemble_kernel(count, place_ref, *refs):
    pieces, out_ref = refs[:count], refs[-1]
    size = pieces[0].shape[0]
    for k, piece in enumerate(pieces):
        copy_strips(piece, 0, out_ref, (place_ref[0] ^ k) * size, size)


def assemble(pieces, place, after=()):
    size, columns = pieces[0].shape
    return pl.pallas_call(
        functools.partial(assemble_kernel, len(pieces)),
        out_shape=jax.ShapeDtypeStruct((size * len(pieces), columns), F32),
        in_specs=[pl.BlockSpec(memory_space=pltpu.SMEM)]
        + [pl.BlockSpec(memory_space=pltpu.VMEM)] * len(pieces)
        + [pl.BlockSpec(memory_space=pl.ANY)] * len(after),
        out_specs=pl.BlockSpec(memory_space=pltpu.VMEM),
        cost_estimate=pl.CostEstimate(
            flops=0,
            bytes_accessed=8 * size * columns * len(pieces),
            transcendentals=0,
        ),
    )(place, *pieces, *after)


def swap(block, axis, distance):
    size = lax.axis_size(axis)
    return lax.ppermute(block, axis, [(i, i ^ distance) for i in range(size)])


def total(parts):
    parts = jnp.stack(parts)
    for axis in ("col", "row"):
        distance = 1
        while distance < lax.axis_size(axis):
            parts = parts + swap(parts, axis, distance)
            distance *= 2
    return parts


def column_dot(first, second):
    return jnp.sum(first * second, axis=0)


def take(whole, place, size):
    return lax.dynamic_slice_in_dim(whole, place, size, 0)


def finish_kernel(coef_ref, right_ref, mask_ref, u_ref, r2_ref, *refs):
    strip = strip_of(u_ref.shape[0])

    def body(s, carry):
        at = pl.ds(pl.multiple_of(s * strip, strip), strip)
        r0 = mask_ref[at, :].astype(F32) * right_ref[at, :]
        value = coef_ref[0] * r0 + coef_ref[1] * u_ref[at, :] + coef_ref[2] * r2_ref[at, :]
        refs[-1][at, :] = value
        return carry

    lax.fori_loop(0, u_ref.shape[0] // strip, body, 0)


def finish(coef, right_side, mask, u, r2, chunk, buffer):
    rows, columns = u.shape
    size = rows // 8
    here = pl.BlockSpec((size, columns), lambda i: (i, chunk))
    own = pl.BlockSpec((size, columns), lambda i: (i, 0))
    given = [] if buffer is None else [buffer]
    return pl.pallas_call(
        finish_kernel,
        out_shape=jax.ShapeDtypeStruct(right_side.shape, F32),
        grid=(8,),
        in_specs=[pl.BlockSpec(coef.shape, lambda i: (0, 0, 0)), here, here, own, own]
        + [pl.BlockSpec(memory_space=pl.ANY)] * len(given),
        out_specs=here,
        input_output_aliases={5: 0} if given else {},
        cost_estimate=pl.CostEstimate(
            flops=6 * rows * columns, bytes_accessed=20 * rows * columns, transcendentals=0
        ),
    )(coef, right_side, mask, u, r2, *given)


def on_device(hessian, right_side, mask, damping):
    n_row, n_col = lax.axis_size("row"), lax.axis_size("col")
    ratio = n_col // n_row
    rows, block = hessian.shape
    piece = rows // n_col
    columns = right_side.shape[1] // CHUNKS
    damping_value = damping[0]
    col = lax.axis_index("col")
    plane, half = col // ratio, col % ratio
    level = lax.axis_index("row")
    own_place = half * block + plane * piece
    at_plane = jnp.stack([plane, half]).astype(jnp.int32)
    at_level = jnp.stack([level]).astype(jnp.int32)
    everyone = range(1, n_row)

    def exchange(pieces):
        return [pieces[0]] + [swap(pieces[k], "col", k * ratio) for k in everyone]

    def place_blocks(pieces, after):
        return assemble(pieces, at_plane, after)

    def home(blocks):
        return lax.psum_scatter(blocks, "row", scatter_dimension=0, tiled=True)

    def to_plane(shard):
        got = exchange([shard] * n_row)
        mine = assemble(got, jnp.zeros_like(at_level))
        return [mine] + [swap(mine, "col", k) for k in range(1, ratio)]

    def turned(shard):
        low, high = jnp.split(shard, 2, axis=1)
        got = [low]
        for k in everyone:
            got.append(swap(jnp.where((level ^ k) < level, low, high), "row", k))
        levels = assemble(got, at_level)
        return levels

    def turned_out(levels, after):
        levels, _ = lax.optimization_barrier((levels, after))
        pieces = [take(levels, (plane ^ k) * piece, piece) for k in range(n_row)]
        return exchange(pieces)

    def form_of(pieces, levels, others, mine):
        levels, pieces = lax.optimization_barrier((levels, pieces))
        others = [take(levels, plane * piece, piece)] + others[1:]
        summed, own = 0.0, 0.0
        for k in range(n_row):
            low, high = jnp.split(pieces[k], 2, axis=1)
            summed += column_dot(jnp.where(plane > level, low, high), others[k])
            own += column_dot(pieces[k], mine[k * piece : (k + 1) * piece])
        zero = jnp.zeros_like(summed)
        pair = jnp.concatenate(
            [
                jnp.where(plane > level, 2.0 * summed, zero),
                jnp.where(plane < level, 2.0 * summed, zero),
            ]
        )
        return jnp.where(plane == level, own, pair)

    def masked(mask_own, summed, own):
        return mask_own * (summed + damping_value * own)

    each = range(CHUNKS)
    cuts = [slice(c * columns, (c + 1) * columns) for c in each]
    mask_all = take(mask, own_place, piece).astype(F32)
    r0_all = mask_all * take(right_side, own_place, piece)
    mask_own = [mask_all[:, cut] for cut in cuts]
    r0_own = [r0_all[:, cut] for cut in cuts]

    def products(inputs, afters, fresh=False):
        pieces, wholes = [], []
        for c in each:
            after = [*afters[c], *(pieces[-1][:1] if c else ())]
            chunk = c if fresh else None
            out = product(hessian, at_plane, inputs[c], columns, piece, chunk, after)
            pieces.append(out[:n_row])
            wholes.extend(out[n_row:])
        return pieces, wholes

    none = [[]] * CHUNKS
    firsts, _ = products([(right_side, mask)] * CHUNKS, none, True)
    got = [exchange(firsts[c]) for c in each]
    blocks = [place_blocks(got[0], firsts[-1][:1])]
    blocks += [place_blocks(got[c], blocks[:1]) for c in each[1:]]
    u_own, gathered = [], []
    for c in each:
        summed = home(blocks[c])
        if c:
            summed, _ = lax.optimization_barrier((summed, gathered[-1][0]))
        u_own.append(masked(mask_own[c], summed, r0_own[c]))
        gathered.append(to_plane(u_own[c]))
    seconds, u = products(gathered, [u_own[1:]] + none[1:])
    got = [exchange(seconds[c]) for c in each]
    blocks = [place_blocks(got[0], seconds[-1][:1])]
    u_late, _ = lax.optimization_barrier((u_own, blocks[0]))
    scalars = total(
        [
            column_dot(r0_all, r0_all),
            jnp.concatenate([column_dot(r0_own[c], u_late[c]) for c in each]),
        ]
    )
    blocks += [place_blocks(got[c], [scalars]) for c in each[1:]]
    kept, gathered, turns = [], [], []
    for c in each:
        n0, c00 = scalars[:, cuts[c]]
        summed = home(blocks[c])
        if c:
            summed, _ = lax.optimization_barrier((summed, turns[-1]))
        uu_own = masked(mask_own[c], summed, u_own[c])
        a0 = n0 / (c00 + epsilon)
        r1_own = r0_own[c] - a0 * u_own[c]
        s1_own = u_own[c] - a0 * uu_own
        n1, c11, c01, c10 = total(
            [
                column_dot(r1_own, r1_own),
                column_dot(r1_own, s1_own),
                column_dot(r0_own[c], s1_own),
                column_dot(r1_own, u_own[c]),
            ]
        )
        b0 = n1 / (n0 + epsilon)
        curve1 = c11 + b0 * (c01 + c10) + b0 * b0 * c00
        a1 = n1 / (curve1 + epsilon)
        t1_own = s1_own + b0 * u_own[c]
        r2_own = r1_own - a1 * t1_own
        kept.append((a0, b0, a1, n1, curve1, t1_own, r2_own))
        gathered.append(to_plane(r2_own))
        turns.append(turned(r2_own))

    afters = [[turns[c]] for c in each]
    others = [turned_out(turns[c], kept[-1][-1]) for c in each]
    afters[0] = afters[0] + [k[-1] for k in kept[1:]]
    thirds, r2 = products(gathered, afters)
    parts = []
    for c in each:
        t1_own, r2_own = kept[c][-2:]
        form = form_of(thirds[c], turns[c], others[c], gathered[c][0])
        parts.append(
            [form, column_dot(r2_own, r2_own), column_dot(r2_own, t1_own)]
        )
    scalars = total([jnp.concatenate(part) for part in zip(*parts)])
    buffer = None
    for c in each:
        a0, b0, a1, n1, curve1, _, _ = kept[c]
        form, n2, cross = scalars[:, cuts[c]]
        b1 = n2 / (n1 + epsilon)
        curve2 = form + damping_value * n2 + 2.0 * b1 * cross + b1 * b1 * curve1
        a2 = n2 / (curve2 + epsilon)
        on_d1 = a1 + a2 * b1
        coef = jnp.stack([a0 + on_d1 * (1.0 + b0), -on_d1 * a0, a2])[:, None, :]
        buffer = finish(coef, right_side, mask, u[c], r2[c], c, buffer)
    return buffer


def solution(mesh):
    in_specs = (P("row", "col"), P("row", None), P("row", None), P())
    out_specs = P("row", None)

    return jax.shard_map(
        on_device, mesh=mesh, in_specs=in_specs, out_specs=out_specs, check_vma=False
    )
```

profile of v0, /device:TPU:0, one launch (start us, length us, event | category | flops | bytes accessed | tf_op | source)
XLA Modules:
  0.0 562.8 jit_solution(84914634714465164)
XLA Ops:
  6.6 26.1 %shard_map.46 = (f32[576,256]{1,0:T(8,128)S(1)}, f32[576,256]{1,0:T(8,128)S(1)}, f32[576,256]{1,0:T(8,128)S(1)}, f32[576,256]{1,0:T(8,128)S(1)}) custom-call(s32[2]{0:T(128)S(1)} %pad_add_fusion.place_ref, f32[4608,2304]{1,0:T(8,128)} %h_ref.11, f32[4608,512]{1,0:T(8,128)} %right_ref.3, s32[4608,512]{1,0:T(8,128)} %mask_ref.3), custom_call_target="tpu_custom_call" | custom-call | flops 16307453952 | bytes 49545216 | tf_op jit(solution)/shard_map/pallas_call | solution.py:129
  32.7 3.0 collective-permute-start
  37.3 26.1 %shard_map.47 = (f32[576,256]{1,0:T(8,128)S(1)}, f32[576,256]{1,0:T(8,128)S(1)}, f32[576,256]{1,0:T(8,128)S(1)}, f32[576,256]{1,0:T(8,128)S(1)}) custom-call(s32[2]{0:T(128)S(1)} %pad_add_fusion.place_ref, f32[4608,2304]{1,0:T(8,128)} %h_ref.11, f32[4608,512]{1,0:T(8,128)} %right_ref.3, s32[4608,512]{1,0:T(8,128)} %mask_ref.3, ...), custom_call_target="tpu_custom_call" | custom-call | flops 16307453952 | bytes 49545216 | tf_op jit(solution)/shard_map/pallas_call | solution.py:129
  65.5 3.3 shard_map.48.refs_4_
  72.4 12.7 %collective-permute-done.3.refs_1_ = f32[576,256]{1,0:T(8,128)S(1)} collective-permute-done((f32[576,256]{1,0:T(8,128)S(1)}, f32[576,256]{1,0:T(8,128)S(1)}, u32[]{:S(2)}, u32[]{:S(2)}) %collective-permute-start.3) | collective-permute-done | bytes 589856 | tf_op jit(solution)/shard_map/ppermute | solution.py:179
  85.2 12.3 %collective-permute-done.4.refs_2_ = f32[576,256]{1,0:T(8,128)S(1)} collective-permute-done((f32[576,256]{1,0:T(8,128)S(1)}, f32[576,256]{1,0:T(8,128)S(1)}, u32[]{:S(2)}, u32[]{:S(2)}) %collective-permute-start.4) | collective-permute-done | bytes 589856 | tf_op jit(solution)/shard_map/ppermute | solution.py:179
  99.1 3.3 shard_map.49
  107.2 11.2 %reduce-scatter.5.cloned.1.call-done = f32[576,256]{1,0:T(8,128)} async-done(((f32[2304,256]{1,0:T(8,128)}), f32[576,256]{1,0:T(8,128)}) %reduce-scatter.5.cloned.1.call-update) | async-done | bytes 589840 | tf_op jit(solution)/shard_map/reduce_scatter | solution.py:255
  123.2 12.7 %collective-permute-done.6.refs_1_ = f32[576,256]{1,0:T(8,128)S(1)} collective-permute-done((f32[576,256]{1,0:T(8,128)S(1)}, f32[576,256]{1,0:T(8,128)S(1)}, u32[]{:S(2)}, u32[]{:S(2)}) %collective-permute-start.6) | collective-permute-done | bytes 589856 | tf_op jit(solution)/shard_map/ppermute | solution.py:179
  135.9 12.3 %collective-permute-done.7.refs_2_ = f32[576,256]{1,0:T(8,128)S(1)} collective-permute-done((f32[576,256]{1,0:T(8,128)S(1)}, f32[576,256]{1,0:T(8,128)S(1)}, u32[]{:S(2)}, u32[]{:S(2)}) %collective-permute-start.7) | collective-permute-done | bytes 589856 | tf_op jit(solution)/shard_map/ppermute | solution.py:179
  149.1 3.3 shard_map.50.refs_0_
  152.3 15.5 %reduce-scatter.7.cloned.1.call-done = f32[576,256]{1,0:T(8,128)} async-done(((f32[2304,256]{1,0:T(8,128)}), f32[576,256]{1,0:T(8,128)}) %reduce-scatter.7.cloned.1.call-update) | async-done | bytes 589840 | tf_op jit(solution)/shard_map/reduce_scatter | solution.py:255
  172.8 12.7 %collective-permute-done.13.refs_1_ = f32[576,256]{1,0:T(8,128)S(1)} collective-permute-done((f32[576,256]{1,0:T(8,128)S(1)}, f32[576,256]{1,0:T(8,128)S(1)}, u32[]{:S(2)}, u32[]{:S(2)}) %collective-permute-start.13) | collective-permute-done | bytes 589856 | tf_op jit(solution)/shard_map/ppermute | solution.py:179
  185.5 12.3 %collective-permute-done.14.refs_2_ = f32[576,256]{1,0:T(8,128)S(1)} collective-permute-done((f32[576,256]{1,0:T(8,128)S(1)}, f32[576,256]{1,0:T(8,128)S(1)}, u32[]{:S(2)}, u32[]{:S(2)}) %collective-permute-start.14) | collective-permute-done | bytes 589856 | tf_op jit(solution)/shard_map/ppermute | solution.py:179
  198.7 3.3 shard_map.52.refs_0_
  203.1 25.7 %shard_map.51 = (f32[576,256]{1,0:T(8,128)S(1)}, f32[576,256]{1,0:T(8,128)S(1)}, f32[576,256]{1,0:T(8,128)S(1)}, f32[576,256]{1,0:T(8,128)S(1)}, f32[4608,256]{1,0:T(8,128)}) custom-call(s32[2]{0:T(128)S(1)} %copy-done.14, f32[4608,2304]{1,0:T(8,128)} %h_ref.11, f32[2304,256]{1,0:T(8,128)S(1)} %copy-done.8, f32[2304,256]{1,0:T(8,128)} %collective-permute-done.9.refs_1_, ...), custom_call_target="tpu_custom_call" | custom-call | flops 16307453952 | bytes 49545216 | tf_op jit(solution)/shard_map/pallas_call | solution.py:129
  233.7 25.6 %shard_map.53 = (f32[576,256]{1,0:T(8,128)S(1)}, f32[576,256]{1,0:T(8,128)S(1)}, f32[576,256]{1,0:T(8,128)S(1)}, f32[576,256]{1,0:T(8,128)S(1)}, f32[4608,256]{1,0:T(8,128)}) custom-call(s32[2]{0:T(128)S(1)} %copy-done.14, f32[4608,2304]{1,0:T(8,128)} %h_ref.11, f32[2304,256]{1,0:T(8,128)S(1)} %copy-done.9, f32[2304,256]{1,0:T(8,128)} %copy-done.60, ...), custom_call_target="tpu_custom_call" | custom-call | flops 16307453952 | bytes 49545216 | tf_op jit(solution)/shard_map/pallas_call | solution.py:129
  261.4 3.3 shard_map.54
  271.5 21.2 %collective-permute-done.18 = f32[2,512]{1,0:T(2,128)S(1)} collective-permute-done((f32[2,512]{1,0:T(2,128)S(1)}, f32[2,512]{1,0:T(2,128)S(1)}, u32[]{:S(2)}, u32[]{:S(2)}) %collective-permute-start.18) | collective-permute-done | bytes 4128 | tf_op jit(solution)/shard_map/ppermute | solution.py:179
  294.2 2.2 collective-permute-done.19
  297.5 3.3 collective-permute-done.20
  302.3 4.4 collective-permute-done.21
  309.0 3.3 shard_map.55
  313.7 2.4 multiply_reduce_fusion.11
  317.4 3.6 collective-permute-done.26
  324.7 3.8 collective-permute-done.28
  329.5 4.8 collective-permute-done.29
  334.9 2.8 multiply_reduce_fusion.4
  343.1 2.7 collective-permute-start.31
  345.8 20.4 %collective-permute-done.30.refs_1_ = f32[576,128]{1,0:T(8,128)} collective-permute-done((f32[576,128]{1,0:T(8,128)S(1)}, f32[576,128]{1,0:T(8,128)}, u32[]{:S(2)}, u32[]{:S(2)}) %collective-permute-start.30) | collective-permute-done | bytes 294944 | tf_op jit(solution)/shard_map/ppermute | solution.py:179
  368.4 11.8 %collective-permute-done.31.refs_2_ = f32[576,128]{1,0:T(8,128)} collective-permute-done((f32[576,128]{1,0:T(8,128)S(1)}, f32[576,128]{1,0:T(8,128)}, u32[]{:S(2)}, u32[]{:S(2)}) %collective-permute-start.31) | collective-permute-done | bytes 294944 | tf_op jit(solution)/shard_map/ppermute | solution.py:179
  380.2 2.5 shard_map.56.refs_2_
  383.5 3.2 shard_map.57.refs_0_
  388.7 2.9 collective-permute-done.33
  399.0 5.8 %collective-permute-start.36 = (f32[4,256]{1,0:T(4,128)S(1)}, f32[4,256]{1,0:T(4,128)S(1)}, u32[]{:S(2)}, u32[]{:S(2)}) collective-permute-start(f32[4,256]{1,0:T(4,128)S(1)} %add.345), channel_id=1, source_target_pairs={{0,8},{8,0},{16,24},{24,16},{1,9},{9,1},{17,25},{25,17},{2,10},{10... | collective-permute-start | bytes 12296 | tf_op jit(solution)/shard_map/ppermute | solution.py:179
  408.4 2.5 collective-permute-done.37
  418.3 5.0 collective-permute-done.45.refs_1_
  423.3 2.4 collective-permute-start.50
  425.7 6.0 %collective-permute-done.46.refs_2_ = f32[576,128]{1,0:T(8,128)} collective-permute-done((f32[576,128]{1,0:T(8,128)}, f32[576,128]{1,0:T(8,128)}, u32[]{:S(2)}, u32[]{:S(2)}) %collective-permute-start.46) | collective-permute-done | bytes 294944 | tf_op jit(solution)/shard_map/ppermute | solution.py:179
  434.5 6.1 %collective-permute-done.47.refs_3_ = f32[576,128]{1,0:T(8,128)} collective-permute-done((f32[576,128]{1,0:T(8,128)}, f32[576,128]{1,0:T(8,128)}, u32[]{:S(2)}, u32[]{:S(2)}) %collective-permute-start.47) | collective-permute-done | bytes 294944 | tf_op jit(solution)/shard_map/ppermute | solution.py:179
  442.0 2.5 shard_map.59.refs_2_
  450.9 3.3 shard_map.60.refs_0_
  454.3 26.4 %shard_map.58 = (f32[576,256]{1,0:T(8,128)S(1)}, f32[576,256]{1,0:T(8,128)S(1)}, f32[576,256]{1,0:T(8,128)S(1)}, f32[576,256]{1,0:T(8,128)S(1)}, f32[4608,256]{1,0:T(8,128)}) custom-call(s32[2]{0:T(128)S(1)} %copy-done.15, f32[4608,2304]{1,0:T(8,128)} %h_ref.11, f32[2304,256]{1,0:T(8,128)} %shard_map.57.refs_0_, ...), custom_call_target="tpu_custom_call" | custom-call | flops 16307453952 | bytes 49545216 | tf_op jit(solution)/shard_map/pallas_call | solution.py:129
  487.9 26.3 %shard_map.61 = (f32[576,256]{1,0:T(8,128)S(1)}, f32[576,256]{1,0:T(8,128)S(1)}, f32[576,256]{1,0:T(8,128)S(1)}, f32[576,256]{1,0:T(8,128)S(1)}, f32[4608,256]{1,0:T(8,128)}) custom-call(s32[2]{0:T(128)S(1)} %copy-done.15, f32[4608,2304]{1,0:T(8,128)} %h_ref.11, f32[2304,256]{1,0:T(8,128)} %shard_map.60.refs_0_, f32[2304,256]{1,0:T(8,128)} %copy-done.59, ...), custom_call_target="tpu_custom_call" | custom-call | flops 16307453952 | bytes 49545216 | tf_op jit(solution)/shard_map/pallas_call | solution.py:129
  525.2 3.6 collective-permute-done.58
  529.8 3.6 collective-permute-done.59
  535.5 10.4 %shard_map.62.refs_0_ = f32[4608,512]{1,0:T(8,128)} custom-call(f32[3,1,256]{2,1,0:T(1,128)} %copy.6.coef_ref, f32[4608,512]{1,0:T(8,128)} %right_ref.3, s32[4608,512]{1,0:T(8,128)} %mask_ref.3, f32[4608,256]{1,0:T(8,128)} %get-tuple-element.91.u_ref, f32[4608,256]{1,0:T(8,128)} %get-tuple-element.92.r2_ref), custom_call_target="tpu_custom_call" | custom-call | flops 7077888 | bytes 23592960 | tf_op jit(solution)/shard_map/pallas_call | solution.py:219
  545.9 10.4 %shard_map.63 = f32[4608,512]{1,0:T(8,128)} custom-call(f32[3,1,256]{2,1,0:T(1,128)} %broadcast_in_dim.4.coef_ref, f32[4608,512]{1,0:T(8,128)} %right_ref.3, s32[4608,512]{1,0:T(8,128)} %mask_ref.3, f32[4608,256]{1,0:T(8,128)} %get-tuple-element.89.u_ref, f32[4608,256]{1,0:T(8,128)} %get-tuple-element.90.r2_ref, ...), custom_call_target="tpu_custom_call", output_to_operand_aliasing={{}: (5, {})} | custom-call | flops 7077888 | bytes 23592960 | tf_op jit(solution)/shard_map/pallas_call | solution.py:219
  (291 shorter events, 114.1 us)
Async XLA Ops:
  6.5 111.9 %reduce-scatter.5.cloned.1.call-start = ((), (), s32[]{:S(2)}) async-start(), calls=%async_computation.4 | async-start | bytes 2949120 | tf_op jit(solution)/shard_map/reduce_scatter | solution.py:255
  32.7 31.6 %collective-permute-start = (f32[576,256]{1,0:T(8,128)S(1)}, f32[576,256]{1,0:T(8,128)S(1)}, u32[]{:S(2)}, u32[]{:S(2)}) collective-permute-start(f32[576,256]{1,0:T(8,128)S(1)} %get-tuple-element.50), channel_id=1, source_target_pairs={{0,2},{1,3},{2,0},{3,1},{4,6},{5,7},{6,4},{7,5},{8,10},{9,11},{10,... | collective-permute-start | bytes 1769480 | tf_op jit(solution)/shard_map/ppermute | solution.py:179
  35.8 28.5 %collective-permute-start.1 = (f32[576,256]{1,0:T(8,128)S(1)}, f32[576,256]{1,0:T(8,128)S(1)}, u32[]{:S(2)}, u32[]{:S(2)}) collective-permute-start(f32[576,256]{1,0:T(8,128)S(1)} %get-tuple-element.51), channel_id=1, source_target_pairs={{0,4},{1,5},{2,6},{3,7},{4,0},{5,1},{6,2},{7,3},{8,12},{9,13},{10,... | collective-permute-start | bytes 1769480 | tf_op jit(solution)/shard_map/ppermute | solution.py:179
  37.3 27.0 %collective-permute-start.2 = (f32[576,256]{1,0:T(8,128)S(1)}, f32[576,256]{1,0:T(8,128)S(1)}, u32[]{:S(2)}, u32[]{:S(2)}) collective-permute-start(f32[576,256]{1,0:T(8,128)S(1)} %get-tuple-element.52), channel_id=1, source_target_pairs={{0,6},{1,7},{2,4},{3,5},{4,2},{5,3},{6,0},{7,1},{8,14},{9,15},{10,... | collective-permute-start | bytes 1769480 | tf_op jit(solution)/shard_map/ppermute | solution.py:179
  68.8 99.0 %reduce-scatter.7.cloned.1.call-start = ((), (), s32[]{:S(2)}) async-start(), calls=%async_computation.5 | async-start | bytes 2949120 | tf_op jit(solution)/shard_map/reduce_scatter | solution.py:255
  68.9 16.3 %collective-permute-start.3 = (f32[576,256]{1,0:T(8,128)S(1)}, f32[576,256]{1,0:T(8,128)S(1)}, u32[]{:S(2)}, u32[]{:S(2)}) collective-permute-start(f32[576,256]{1,0:T(8,128)S(1)} %get-tuple-element.54), channel_id=1, source_target_pairs={{0,2},{1,3},{2,0},{3,1},{4,6},{5,7},{6,4},{7,5},{8,10},{9,11},{10,... | collective-permute-start | bytes 1769480 | tf_op jit(solution)/shard_map/ppermute | solution.py:179
  70.9 26.6 %collective-permute-start.4 = (f32[576,256]{1,0:T(8,128)S(1)}, f32[576,256]{1,0:T(8,128)S(1)}, u32[]{:S(2)}, u32[]{:S(2)}) collective-permute-start(f32[576,256]{1,0:T(8,128)S(1)} %get-tuple-element.55), channel_id=1, source_target_pairs={{0,4},{1,5},{2,6},{3,7},{4,0},{5,1},{6,2},{7,3},{8,12},{9,13},{10,... | collective-permute-start | bytes 1769480 | tf_op jit(solution)/shard_map/ppermute | solution.py:179
  72.4 25.1 %collective-permute-start.5 = (f32[576,256]{1,0:T(8,128)S(1)}, f32[576,256]{1,0:T(8,128)S(1)}, u32[]{:S(2)}, u32[]{:S(2)}) collective-permute-start(f32[576,256]{1,0:T(8,128)S(1)} %get-tuple-element.56), channel_id=1, source_target_pairs={{0,6},{1,7},{2,4},{3,5},{4,2},{5,3},{6,0},{7,1},{8,14},{9,15},{10,... | collective-permute-start | bytes 1769480 | tf_op jit(solution)/shard_map/ppermute | solution.py:179
  102.5 210.5 %reduce-scatter.11.cloned.1.call-start = ((), (), s32[]{:S(2)}) async-start(), calls=%async_computation.7 | async-start | bytes 2949120 | tf_op jit(solution)/shard_map/reduce_scatter | solution.py:255
  119.7 16.3 %collective-permute-start.6 = (f32[576,256]{1,0:T(8,128)S(1)}, f32[576,256]{1,0:T(8,128)S(1)}, u32[]{:S(2)}, u32[]{:S(2)}) collective-permute-start(f32[576,256]{1,0:T(8,128)S(1)} %add_multiply_fusion.1.refs_0_), channel_id=1, source_target_pairs={{0,2},{1,3},{2,0},{3,1},{4,6},{5,7},{6,4},{7,5},{8,10},{9,11},{10,... | collective-permute-start | bytes 1769480 | tf_op jit(solution)/shard_map/ppermute | solution.py:179
  121.2 27.0 %collective-permute-start.7 = (f32[576,256]{1,0:T(8,128)S(1)}, f32[576,256]{1,0:T(8,128)S(1)}, u32[]{:S(2)}, u32[]{:S(2)}) collective-permute-start(f32[576,256]{1,0:T(8,128)S(1)} %add_multiply_fusion.1.refs_0_), channel_id=1, source_target_pairs={{0,4},{1,5},{2,6},{3,7},{4,0},{5,1},{6,2},{7,3},{8,12},{9,13},{10,... | collective-permute-start | bytes 1769480 | tf_op jit(solution)/shard_map/ppermute | solution.py:179
  122.7 26.4 %collective-permute-start.8 = (f32[576,256]{1,0:T(8,128)S(1)}, f32[576,256]{1,0:T(8,128)}, u32[]{:S(2)}, u32[]{:S(2)}) collective-permute-start(f32[576,256]{1,0:T(8,128)S(1)} %add_multiply_fusion.1.refs_0_), channel_id=1, source_target_pairs={{0,6},{1,7},{2,4},{3,5},{4,2},{5,3},{6,0},{7,1},{8,14},{9,15},{10,... | collective-permute-start | bytes 1769480 | tf_op jit(solution)/shard_map/ppermute | solution.py:179
  152.3 49.7 %collective-permute-start.9 = (f32[2304,256]{1,0:T(8,128)}, f32[2304,256]{1,0:T(8,128)}, u32[]{:S(2)}, u32[]{:S(2)}) collective-permute-start(f32[2304,256]{1,0:T(8,128)} %shard_map.50.refs_0_), channel_id=1, source_target_pairs={{0,1},{1,0},{2,3},{3,2},{4,5},{5,4},{6,7},{7,6},{8,9},{9,8},{10,11... | collective-permute-start | bytes 7077896 | tf_op jit(solution)/shard_map/ppermute | solution.py:179
  169.2 16.3 %collective-permute-start.13 = (f32[576,256]{1,0:T(8,128)S(1)}, f32[576,256]{1,0:T(8,128)S(1)}, u32[]{:S(2)}, u32[]{:S(2)}) collective-permute-start(f32[576,256]{1,0:T(8,128)S(1)} %add_multiply_fusion.refs_2_.refs_0_), channel_id=1, source_target_pairs={{0,2},{1,3},{2,0},{3,1},{4,6},{5,7},{6,4},{7,5},{8,10},{9,11},{10,... | collective-permute-start | bytes 1769480 | tf_op jit(solution)/shard_map/ppermute | solution.py:179
  170.8 27.1 %collective-permute-start.14 = (f32[576,256]{1,0:T(8,128)S(1)}, f32[576,256]{1,0:T(8,128)S(1)}, u32[]{:S(2)}, u32[]{:S(2)}) collective-permute-start(f32[576,256]{1,0:T(8,128)S(1)} %add_multiply_fusion.refs_2_.refs_0_), channel_id=1, source_target_pairs={{0,4},{1,5},{2,6},{3,7},{4,0},{5,1},{6,2},{7,3},{8,12},{9,13},{10,... | collective-permute-start | bytes 1769480 | tf_op jit(solution)/shard_map/ppermute | solution.py:179
  172.3 26.4 %collective-permute-start.15 = (f32[576,256]{1,0:T(8,128)S(1)}, f32[576,256]{1,0:T(8,128)}, u32[]{:S(2)}, u32[]{:S(2)}) collective-permute-start(f32[576,256]{1,0:T(8,128)S(1)} %add_multiply_fusion.refs_2_.refs_0_), channel_id=1, source_target_pairs={{0,6},{1,7},{2,4},{3,5},{4,2},{5,3},{6,0},{7,1},{8,14},{9,15},{10,... | collective-permute-start | bytes 1769480 | tf_op jit(solution)/shard_map/ppermute | solution.py:179
  202.0 30.3 %collective-permute-start.16 = (f32[2304,256]{1,0:T(8,128)}, f32[2304,256]{1,0:T(8,128)S(1)}, u32[]{:S(2)}, u32[]{:S(2)}) collective-permute-start(f32[2304,256]{1,0:T(8,128)} %shard_map.52.refs_0_), channel_id=1, source_target_pairs={{0,1},{1,0},{2,3},{3,2},{4,5},{5,4},{6,7},{7,6},{8,9},{9,8},{10,11... | collective-permute-start | bytes 7077896 | tf_op jit(solution)/shard_map/ppermute | solution.py:179
  228.8 31.4 %collective-permute-start.10 = (f32[576,256]{1,0:T(8,128)S(1)}, f32[576,256]{1,0:T(8,128)S(1)}, u32[]{:S(2)}, u32[]{:S(2)}) collective-permute-start(f32[576,256]{1,0:T(8,128)S(1)} %get-tuple-element.59), channel_id=1, source_target_pairs={{0,2},{1,3},{2,0},{3,1},{4,6},{5,7},{6,4},{7,5},{8,10},{9,11},{10,... | collective-permute-start | bytes 1769480 | tf_op jit(solution)/shard_map/ppermute | solution.py:179
  229.2 30.9 %collective-permute-start.11 = (f32[576,256]{1,0:T(8,128)S(1)}, f32[576,256]{1,0:T(8,128)S(1)}, u32[]{:S(2)}, u32[]{:S(2)}) collective-permute-start(f32[576,256]{1,0:T(8,128)S(1)} %get-tuple-element.60), channel_id=1, source_target_pairs={{0,4},{1,5},{2,6},{3,7},{4,0},{5,1},{6,2},{7,3},{8,12},{9,13},{10,... | collective-permute-start | bytes 1769480 | tf_op jit(solution)/shard_map/ppermute | solution.py:179
  230.8 29.3 %collective-permute-start.12 = (f32[576,256]{1,0:T(8,128)S(1)}, f32[576,256]{1,0:T(8,128)S(1)}, u32[]{:S(2)}, u32[]{:S(2)}) collective-permute-start(f32[576,256]{1,0:T(8,128)S(1)} %get-tuple-element.61), channel_id=1, source_target_pairs={{0,6},{1,7},{2,4},{3,5},{4,2},{5,3},{6,0},{7,1},{8,14},{9,15},{10,... | collective-permute-start | bytes 1769480 | tf_op jit(solution)/shard_map/ppermute | solution.py:179
  264.7 118.0 %reduce-scatter.9.cloned.1.call-start = ((), (), s32[]{:S(2)}) async-start(), calls=%async_computation.6 | async-start | bytes 2949120 | tf_op jit(solution)/shard_map/reduce_scatter | solution.py:255
  264.9 42.4 %collective-permute-start.22 = (f32[576,256]{1,0:T(8,128)S(1)}, f32[576,256]{1,0:T(8,128)S(1)}, u32[]{:S(2)}, u32[]{:S(2)}) collective-permute-start(f32[576,256]{1,0:T(8,128)S(1)} %get-tuple-element.65), channel_id=1, source_target_pairs={{0,2},{1,3},{2,0},{3,1},{4,6},{5,7},{6,4},{7,5},{8,10},{9,11},{10,... | collective-permute-start | bytes 1769480 | tf_op jit(solution)/shard_map/ppermute | solution.py:179
  265.5 41.9 %collective-permute-start.23 = (f32[576,256]{1,0:T(8,128)S(1)}, f32[576,256]{1,0:T(8,128)S(1)}, u32[]{:S(2)}, u32[]{:S(2)}) collective-permute-start(f32[576,256]{1,0:T(8,128)S(1)} %get-tuple-element.66), channel_id=1, source_target_pairs={{0,4},{1,5},{2,6},{3,7},{4,0},{5,1},{6,2},{7,3},{8,12},{9,13},{10,... | collective-permute-start | bytes 1769480 | tf_op jit(solution)/shard_map/ppermute | solution.py:179
  267.0 41.9 %collective-permute-start.24 = (f32[576,256]{1,0:T(8,128)S(1)}, f32[576,256]{1,0:T(8,128)}, u32[]{:S(2)}, u32[]{:S(2)}) collective-permute-start(f32[576,256]{1,0:T(8,128)S(1)} %get-tuple-element.67), channel_id=1, source_target_pairs={{0,6},{1,7},{2,4},{3,5},{4,2},{5,3},{6,0},{7,1},{8,14},{9,15},{10,... | collective-permute-start | bytes 1769480 | tf_op jit(solution)/shard_map/ppermute | solution.py:179
  271.0 21.7 %collective-permute-start.18 = (f32[2,512]{1,0:T(2,128)S(1)}, f32[2,512]{1,0:T(2,128)S(1)}, u32[]{:S(2)}, u32[]{:S(2)}) collective-permute-start(f32[2,512]{1,0:T(2,128)S(1)} %fusion.16), channel_id=1, source_target_pairs={{0,2},{1,3},{2,0},{3,1},{4,6},{5,7},{6,4},{7,5},{8,10},{9,11},{10,... | collective-permute-start | bytes 12296 | tf_op jit(solution)/shard_map/ppermute | solution.py:179
  300.7 6.0 %collective-permute-start.21 = (f32[2,512]{1,0:T(2,128)S(1)}, f32[2,512]{1,0:T(2,128)S(1)}, u32[]{:S(2)}, u32[]{:S(2)}) collective-permute-start(f32[2,512]{1,0:T(2,128)S(1)} %add.326), channel_id=1, source_target_pairs={{0,16},{8,24},{16,0},{24,8},{1,17},{9,25},{17,1},{25,9},{2,18},{10... | collective-permute-start | bytes 12296 | tf_op jit(solution)/shard_map/ppermute | solution.py:179
  328.5 5.8 %collective-permute-start.29 = (f32[4,256]{1,0:T(4,128)S(1)}, f32[4,256]{1,0:T(4,128)S(1)}, u32[]{:S(2)}, u32[]{:S(2)}) collective-permute-start(f32[4,256]{1,0:T(4,128)S(1)} %add.334), channel_id=1, source_target_pairs={{0,16},{8,24},{16,0},{24,8},{1,17},{9,25},{17,1},{25,9},{2,18},{10... | collective-permute-start | bytes 12296 | tf_op jit(solution)/shard_map/ppermute | solution.py:179
  339.6 26.6 %collective-permute-start.30 = (f32[576,128]{1,0:T(8,128)S(1)}, f32[576,128]{1,0:T(8,128)}, u32[]{:S(2)}, u32[]{:S(2)}) collective-permute-start(f32[576,128]{1,0:T(8,128)S(1)} %get-tuple-element.151), channel_id=1, source_target_pairs={{0,8},{8,0},{16,24},{24,16},{1,9},{9,1},{17,25},{25,17},{2,10},{10... | collective-permute-start | bytes 884744 | tf_op jit(solution)/shard_map/ppermute | solution.py:179
  339.6 43.0 %collective-permute-start.38 = (f32[576,256]{1,0:T(8,128)}, f32[576,256]{1,0:T(8,128)S(1)}, u32[]{:S(2)}, u32[]{:S(2)}) collective-permute-start(f32[576,256]{1,0:T(8,128)} %get-tuple-element.125.refs_0_), channel_id=1, source_target_pairs={{0,2},{1,3},{2,0},{3,1},{4,6},{5,7},{6,4},{7,5},{8,10},{9,11},{10,... | collective-permute-start | bytes 1769480 | tf_op jit(solution)/shard_map/ppermute | solution.py:179
  340.7 42.0 %collective-permute-start.39 = (f32[576,256]{1,0:T(8,128)}, f32[576,256]{1,0:T(8,128)}, u32[]{:S(2)}, u32[]{:S(2)}) collective-permute-start(f32[576,256]{1,0:T(8,128)} %get-tuple-element.125.refs_0_), channel_id=1, source_target_pairs={{0,4},{1,5},{2,6},{3,7},{4,0},{5,1},{6,2},{7,3},{8,12},{9,13},{10,... | collective-permute-start | bytes 1769480 | tf_op jit(solution)/shard_map/ppermute | solution.py:179
  342.1 40.5 %collective-permute-start.40 = (f32[576,256]{1,0:T(8,128)}, f32[576,256]{1,0:T(8,128)}, u32[]{:S(2)}, u32[]{:S(2)}) collective-permute-start(f32[576,256]{1,0:T(8,128)} %get-tuple-element.125.refs_0_), channel_id=1, source_target_pairs={{0,6},{1,7},{2,4},{3,5},{4,2},{5,3},{6,0},{7,1},{8,14},{9,15},{10,... | collective-permute-start | bytes 1769480 | tf_op jit(solution)/shard_map/ppermute | solution.py:179
  343.1 37.1 %collective-permute-start.31 = (f32[576,128]{1,0:T(8,128)S(1)}, f32[576,128]{1,0:T(8,128)}, u32[]{:S(2)}, u32[]{:S(2)}) collective-permute-start(f32[576,128]{1,0:T(8,128)S(1)} %get-tuple-element.150), channel_id=1, source_target_pairs={{0,16},{8,24},{16,0},{24,8},{1,17},{9,25},{17,1},{25,9},{2,18},{10... | collective-permute-start | bytes 884744 | tf_op jit(solution)/shard_map/ppermute | solution.py:179
  366.2 14.0 %collective-permute-start.32 = (f32[576,128]{1,0:T(8,128)S(1)}, f32[576,128]{1,0:T(8,128)}, u32[]{:S(2)}, u32[]{:S(2)}) collective-permute-start(f32[576,128]{1,0:T(8,128)S(1)} %get-tuple-element.149), channel_id=1, source_target_pairs={{0,24},{8,16},{16,8},{24,0},{1,25},{9,17},{17,9},{25,1},{2,26},{10... | collective-permute-start | bytes 884744 | tf_op jit(solution)/shard_map/ppermute | solution.py:179
  386.7 67.5 %collective-permute-start.41 = (f32[2304,256]{1,0:T(8,128)}, f32[2304,256]{1,0:T(8,128)}, u32[]{:S(2)}, u32[]{:S(2)}) collective-permute-start(f32[2304,256]{1,0:T(8,128)} %shard_map.57.refs_0_), channel_id=1, source_target_pairs={{0,1},{1,0},{2,3},{3,2},{4,5},{5,4},{6,7},{7,6},{8,9},{9,8},{10,11... | collective-permute-start | bytes 7077896 | tf_op jit(solution)/shard_map/ppermute | solution.py:179
  399.0 7.4 %collective-permute-start.36 = (f32[4,256]{1,0:T(4,128)S(1)}, f32[4,256]{1,0:T(4,128)S(1)}, u32[]{:S(2)}, u32[]{:S(2)}) collective-permute-start(f32[4,256]{1,0:T(4,128)S(1)} %add.345), channel_id=1, source_target_pairs={{0,8},{8,0},{16,24},{24,16},{1,9},{9,1},{17,25},{25,17},{2,10},{10... | collective-permute-start | bytes 12296 | tf_op jit(solution)/shard_map/ppermute | solution.py:179
  413.3 10.0 %collective-permute-start.45 = (f32[576,128]{1,0:T(8,128)S(1)}, f32[576,128]{1,0:T(8,128)}, u32[]{:S(2)}, u32[]{:S(2)}) collective-permute-start(f32[576,128]{1,0:T(8,128)S(1)} %get-tuple-element.147), channel_id=1, source_target_pairs={{0,8},{8,0},{16,24},{24,16},{1,9},{9,1},{17,25},{25,17},{2,10},{10... | collective-permute-start | bytes 884744 | tf_op jit(solution)/shard_map/ppermute | solution.py:179
  415.4 16.3 %collective-permute-start.46 = (f32[576,128]{1,0:T(8,128)}, f32[576,128]{1,0:T(8,128)}, u32[]{:S(2)}, u32[]{:S(2)}) collective-permute-start(f32[576,128]{1,0:T(8,128)} %get-tuple-element.146), channel_id=1, source_target_pairs={{0,16},{8,24},{16,0},{24,8},{1,17},{9,25},{17,1},{25,9},{2,18},{10... | collective-permute-start | bytes 884744 | tf_op jit(solution)/shard_map/ppermute | solution.py:179
  415.4 31.2 %collective-permute-start.48 = (f32[576,256]{1,0:T(8,128)S(1)}, f32[576,256]{1,0:T(8,128)S(1)}, u32[]{:S(2)}, u32[]{:S(2)}) collective-permute-start(f32[576,256]{1,0:T(8,128)S(1)} %get-tuple-element.126.refs_3_.refs_0_), channel_id=1, source_target_pairs={{0,2},{1,3},{2,0},{3,1},{4,6},{5,7},{6,4},{7,5},{8,10},{9,11},{10,... | collective-permute-start | bytes 1769480 | tf_op jit(solution)/shard_map/ppermute | solution.py:179
  416.8 31.2 %collective-permute-start.49 = (f32[576,256]{1,0:T(8,128)S(1)}, f32[576,256]{1,0:T(8,128)S(1)}, u32[]{:S(2)}, u32[]{:S(2)}) collective-permute-start(f32[576,256]{1,0:T(8,128)S(1)} %get-tuple-element.126.refs_3_.refs_0_), channel_id=1, source_target_pairs={{0,4},{1,5},{2,6},{3,7},{4,0},{5,1},{6,2},{7,3},{8,12},{9,13},{10,... | collective-permute-start | bytes 1769480 | tf_op jit(solution)/shard_map/ppermute | solution.py:179
  423.3 25.3 %collective-permute-start.50 = (f32[576,256]{1,0:T(8,128)S(1)}, f32[576,256]{1,0:T(8,128)S(1)}, u32[]{:S(2)}, u32[]{:S(2)}) collective-permute-start(f32[576,256]{1,0:T(8,128)S(1)} %get-tuple-element.126.refs_3_.refs_0_), channel_id=1, source_target_pairs={{0,6},{1,7},{2,4},{3,5},{4,2},{5,3},{6,0},{7,1},{8,14},{9,15},{10,... | collective-permute-start | bytes 1769480 | tf_op jit(solution)/shard_map/ppermute | solution.py:179
  431.7 8.8 %collective-permute-start.47 = (f32[576,128]{1,0:T(8,128)}, f32[576,128]{1,0:T(8,128)}, u32[]{:S(2)}, u32[]{:S(2)}) collective-permute-start(f32[576,128]{1,0:T(8,128)} %get-tuple-element.145), channel_id=1, source_target_pairs={{0,24},{8,16},{16,8},{24,0},{1,25},{9,17},{17,9},{25,1},{2,26},{10... | collective-permute-start | bytes 884744 | tf_op jit(solution)/shard_map/ppermute | solution.py:179
  440.5 40.2 %collective-permute-start.42 = (f32[576,128]{1,0:T(8,128)}, f32[576,128]{1,0:T(8,128)}, u32[]{:S(2)}, u32[]{:S(2)}) collective-permute-start(f32[576,128]{1,0:T(8,128)} %get-tuple-element.139), channel_id=1, source_target_pairs={{0,2},{1,3},{2,0},{3,1},{4,6},{5,7},{6,4},{7,5},{8,10},{9,11},{10,... | collective-permute-start | bytes 884744 | tf_op jit(solution)/shard_map/ppermute | solution.py:179
  446.6 36.8 %collective-permute-start.43 = (f32[576,128]{1,0:T(8,128)}, f32[576,128]{1,0:T(8,128)}, u32[]{:S(2)}, u32[]{:S(2)}) collective-permute-start(f32[576,128]{1,0:T(8,128)} %get-tuple-element.141), channel_id=1, source_target_pairs={{0,4},{1,5},{2,6},{3,7},{4,0},{5,1},{6,2},{7,3},{8,12},{9,13},{10,... | collective-permute-start | bytes 884744 | tf_op jit(solution)/shard_map/ppermute | solution.py:179
  448.1 37.0 %collective-permute-start.44 = (f32[576,128]{1,0:T(8,128)}, f32[576,128]{1,0:T(8,128)}, u32[]{:S(2)}, u32[]{:S(2)}) collective-permute-start(f32[576,128]{1,0:T(8,128)} %get-tuple-element.140), channel_id=1, source_target_pairs={{0,6},{1,7},{2,4},{3,5},{4,2},{5,3},{6,0},{7,1},{8,14},{9,15},{10,... | collective-permute-start | bytes 884744 | tf_op jit(solution)/shard_map/ppermute | solution.py:179
  449.5 64.8 %collective-permute-start.52 = (f32[576,128]{1,0:T(8,128)}, f32[576,128]{1,0:T(8,128)}, u32[]{:S(2)}, u32[]{:S(2)}) collective-permute-start(f32[576,128]{1,0:T(8,128)} %get-tuple-element.142), channel_id=1, source_target_pairs={{0,2},{1,3},{2,0},{3,1},{4,6},{5,7},{6,4},{7,5},{8,10},{9,11},{10,... | collective-permute-start | bytes 884744 | tf_op jit(solution)/shard_map/ppermute | solution.py:179
  454.2 32.3 %collective-permute-start.51 = (f32[2304,256]{1,0:T(8,128)}, f32[2304,256]{1,0:T(8,128)S(1)}, u32[]{:S(2)}, u32[]{:S(2)}) collective-permute-start(f32[2304,256]{1,0:T(8,128)} %shard_map.60.refs_0_), channel_id=1, source_target_pairs={{0,1},{1,0},{2,3},{3,2},{4,5},{5,4},{6,7},{7,6},{8,9},{9,8},{10,11... | collective-permute-start | bytes 7077896 | tf_op jit(solution)/shard_map/ppermute | solution.py:179
  480.8 34.7 %collective-permute-start.53 = (f32[576,128]{1,0:T(8,128)S(1)}, f32[576,128]{1,0:T(8,128)S(1)}, u32[]{:S(2)}, u32[]{:S(2)}) collective-permute-start(f32[576,128]{1,0:T(8,128)S(1)} %copy-done.44), channel_id=1, source_target_pairs={{0,4},{1,5},{2,6},{3,7},{4,0},{5,1},{6,2},{7,3},{8,12},{9,13},{10,... | collective-permute-start | bytes 884744 | tf_op jit(solution)/shard_map/ppermute | solution.py:179
  483.4 33.0 %collective-permute-start.54 = (f32[576,128]{1,0:T(8,128)S(1)}, f32[576,128]{1,0:T(8,128)S(1)}, u32[]{:S(2)}, u32[]{:S(2)}) collective-permute-start(f32[576,128]{1,0:T(8,128)S(1)} %copy-done.43), channel_id=1, source_target_pairs={{0,6},{1,7},{2,4},{3,5},{4,2},{5,3},{6,0},{7,1},{8,14},{9,15},{10,... | collective-permute-start | bytes 884744 | tf_op jit(solution)/shard_map/ppermute | solution.py:179
  (77 other events, 949.1 us)
Sparse Core Ops, SparseCore 0:
  69.0 49.3 reduce-scatter.4
  120.7 47.0 reduce-scatter.6
  264.8 46.6 reduce-scatter.10
  313.7 63.9 reduce-scatter.8
where the time goes:
time: 565 us; the launch traced here: 563 us
  waiting for transfers between devices  222 us (39%)
  Pallas kernels  208 us (37%)
  starting transfers between devices  69.7 us (12%)
  other arithmetic  27.5 us (5%)
  local copies, waits for them, and re-layouts  20.6 us (4%)
  between operations  14.4 us (3%)
    ppermute x60, waiting for transfers between devices, swap(): return lax.ppermute(block, axis, [(i, i ^ distance) for i in range(size)])  196 us
    pallas_call x6, Pallas kernels, product(): pl.pallas_call(functools.partial(product_kernel, layout), out_shape=out_s...  156 us
    ppermute x60, starting transfers between devices, swap(): return lax.ppermute(block, axis, [(i, i ^ distance) for i in range(size)])  69.2 us
    pallas_call x10, Pallas kernels, assemble(): pl.pallas_call(functools.partial(assemble_kernel, len(pieces)), out_shape...  31.2 us
    reduce_scatter x4, waiting for transfers between devices, home(): return lax.psum_scatter(blocks, 'row', scatter_dimension=0, tiled=True)  26.7 us
    pallas_call x2, Pallas kernels, finish(): pl.pallas_call(finish_kernel, out_shape=jax.ShapeDtypeStruct(right_side.s...  20.8 us
    unnamed x122, local copies, waits for them, and re-layouts  16.3 us
    reduce_sum x16, other arithmetic, column_dot(): return jnp.sum(first * second, axis=0)  15.9 us
  transfers between devices with their start and end apart: 64, of which 33 were waited for; matrix products, arithmetic and copies ran while one was open for 5% of the time, Pallas kernels for 27%

commit v1 on v0

--- a/solution.py
+++ b/solution.py
@@ -174,6 +174,37 @@
     )(place, *pieces, *after)
 
 
+def turn_kernel(count, place_ref, *refs):
+    groups = (len(refs) - 1) // (2 * count)
+    inputs = refs[: groups * count]
+    outputs = refs[-groups * count :]
+    for group in range(groups):
+        for j in range(count):
+            for k in range(count):
+
+                @pl.when((place_ref[0] ^ j) == k)
+                def _(group=group, j=j, k=k):
+                    source, target = inputs[group * count + k], outputs[group * count + j]
+                    copy_strips(source, 0, target, 0, source.shape[0])
+
+
+def turn(groups, place, after):
+    count = len(groups[0])
+    flat = [x for group in groups for x in group]
+    out = pl.pallas_call(
+        functools.partial(turn_kernel, count),
+        out_shape=[jax.ShapeDtypeStruct(x.shape, F32) for x in flat],
+        in_specs=[pl.BlockSpec(memory_space=pltpu.SMEM)]
+        + [pl.BlockSpec(memory_space=pltpu.VMEM)] * len(flat)
+        + [pl.BlockSpec(memory_space=pl.ANY)],
+        out_specs=[pl.BlockSpec(memory_space=pltpu.VMEM)] * len(flat),
+        cost_estimate=pl.CostEstimate(
+            flops=0, bytes_accessed=8 * len(flat) * flat[0].size, transcendentals=0
+        ),
+    )(place, *flat, after)
+    return [out[g * count : (g + 1) * count] for g in range(len(groups))]
+
+
 def swap(block, axis, distance):
     size = lax.axis_size(axis)
     return lax.ppermute(block, axis, [(i, i ^ distance) for i in range(size)])
@@ -259,22 +290,14 @@
         mine = assemble(got, jnp.zeros_like(at_level))
         return [mine] + [swap(mine, "col", k) for k in range(1, ratio)]
 
-    def turned(shard):
+    def levels_of(shard):
         low, high = jnp.split(shard, 2, axis=1)
         got = [low]
         for k in everyone:
             got.append(swap(jnp.where((level ^ k) < level, low, high), "row", k))
-        levels = assemble(got, at_level)
-        return levels
-
-    def turned_out(levels, after):
-        levels, _ = lax.optimization_barrier((levels, after))
-        pieces = [take(levels, (plane ^ k) * piece, piece) for k in range(n_row)]
-        return exchange(pieces)
-
-    def form_of(pieces, levels, others, mine):
-        levels, pieces = lax.optimization_barrier((levels, pieces))
-        others = [take(levels, plane * piece, piece)] + others[1:]
+        return got
+
+    def form_of(pieces, others, mine):
         summed, own = 0.0, 0.0
         for k in range(n_row):
             low, high = jnp.split(pieces[k], 2, axis=1)
@@ -332,55 +355,71 @@
         ]
     )
     blocks += [place_blocks(got[c], [scalars]) for c in each[1:]]
-    kept, gathered, turns = [], [], []
+
+    def hold(value, *others):
+        return lax.optimization_barrier((value, others))[0]
+
+    kept, gathered = [], []
     for c in each:
         n0, c00 = scalars[:, cuts[c]]
         summed = home(blocks[c])
         if c:
-            summed, _ = lax.optimization_barrier((summed, turns[-1]))
+            summed = hold(summed, gathered[-1][0])
         uu_own = masked(mask_own[c], summed, u_own[c])
         a0 = n0 / (c00 + epsilon)
         r1_own = r0_own[c] - a0 * u_own[c]
         s1_own = u_own[c] - a0 * uu_own
-        n1, c11, c01, c10 = total(
-            [
-                column_dot(r1_own, r1_own),
-                column_dot(r1_own, s1_own),
-                column_dot(r0_own[c], s1_own),
-                column_dot(r1_own, u_own[c]),
-            ]
+        w_own = r1_own - a0 * s1_own
+        gathered.append(to_plane(w_own))
+        kept.append((a0, gathered[c][0], r1_own, s1_own, w_own, uu_own))
+    w_last = kept[-1][4]
+    got = [levels_of(hold(kept[c][4], w_last)) for c in each]
+    others, thirds, w = [], [], []
+    for c in each:
+        after = [w_last]
+        if c:
+            turned = turn(got, jnp.stack([level ^ plane]), thirds[0][0])
+            others = [exchange(turned[d]) for d in each]
+            after = [turned[-1][0]]
+        *pieces, whole = product(
+            hessian, at_plane, gathered[c], columns, piece, after=after
         )
+        thirds.append(pieces)
+        w.append(whole)
+    rows_of = []
+    for c in each:
+        a0, mine, r1, s1, w_own, uu = kept[c]
+        u_c = u_own[c]
+        form = form_of(thirds[c], others[c], mine)
+        pairs = (
+            (r1, r1), (r1, s1), (r0_own[c], s1), (r1, u_c), (w_own, w_own), (w_own, r1),
+            (w_own, u_c), (w_own, s1), (w_own, uu), (u_c, uu), (u_c, u_c), (u_c, s1),
+        )
+        rows_of.append([form] + [column_dot(*pair) for pair in pairs])
+    sums = total([jnp.concatenate(part) for part in zip(*rows_of)])
+    buffer = None
+    for c in each:
+        n0, c00 = scalars[:, cuts[c]]
+        a0 = kept[c][0]
+        form, n1, c11, c01, c10, ww, wr, wu, ws, wuu, uuu, u2, us = sums[:, cuts[c]]
         b0 = n1 / (n0 + epsilon)
         curve1 = c11 + b0 * (c01 + c10) + b0 * b0 * c00
         a1 = n1 / (curve1 + epsilon)
-        t1_own = s1_own + b0 * u_own[c]
-        r2_own = r1_own - a1 * t1_own
-        kept.append((a0, b0, a1, n1, curve1, t1_own, r2_own))
-        gathered.append(to_plane(r2_own))
-        turns.append(turned(r2_own))
-
-    afters = [[turns[c]] for c in each]
-    others = [turned_out(turns[c], kept[-1][-1]) for c in each]
-    afters[0] = afters[0] + [k[-1] for k in kept[1:]]
-    thirds, r2 = products(gathered, afters)
-    parts = []
-    for c in each:
-        t1_own, r2_own = kept[c][-2:]
-        form = form_of(thirds[c], turns[c], others[c], gathered[c][0])
-        parts.append(
-            [form, column_dot(r2_own, r2_own), column_dot(r2_own, t1_own)]
-        )
-    scalars = total([jnp.concatenate(part) for part in zip(*parts)])
-    buffer = None
-    for c in each:
-        a0, b0, a1, n1, curve1, _, _ = kept[c]
-        form, n2, cross = scalars[:, cuts[c]]
+        c2 = jnp.where(a0 > 0.0, a1 / jnp.where(a0 > 0.0, a0, 1.0), 0.0)
+        c1, c3 = 1.0 - c2, -a1 * b0
+        n2 = c1 * c1 * n1 + c2 * c2 * ww + c3 * c3 * u2
+        n2 = n2 + 2.0 * (c1 * c2 * wr + c1 * c3 * c10 + c2 * c3 * wu)
+        n2 = jnp.maximum(n2, 0.0)
+        cross = c1 * (c11 + b0 * c10) + c2 * (ws + b0 * wu) + c3 * (us + b0 * u2)
+        curve2 = c2 * c2 * (form + damping_value * ww) + c1 * c1 * c11 + c3 * c3 * uuu
+        curve2 = curve2 + 2.0 * (c1 * c2 * ws + c2 * c3 * wuu + c1 * c3 * us)
         b1 = n2 / (n1 + epsilon)
-        curve2 = form + damping_value * n2 + 2.0 * b1 * cross + b1 * b1 * curve1
-        a2 = n2 / (curve2 + epsilon)
+        curve2 = curve2 + 2.0 * b1 * cross + b1 * b1 * curve1
+        a2 = n2 / (jnp.maximum(curve2, damping_value * n2) + epsilon)
         on_d1 = a1 + a2 * b1
-        coef = jnp.stack([a0 + on_d1 * (1.0 + b0), -on_d1 * a0, a2])[:, None, :]
-        buffer = finish(coef, right_side, mask, u[c], r2[c], c, buffer)
+        on_r1 = on_d1 + a2 * c1
+        coef = jnp.stack([a0 + on_d1 * b0 + on_r1, a2 * c3 - a0 * on_r1, a2 * c2])
+        buffer = finish(coef[:, None, :], right_side, mask, u[c], w[c], c, buffer)
     return buffer
 
 

time: 565 us -> 535 us (0.947)
  starting transfers between devices: 69.7 us -> 54.5 us
  waiting for transfers between devices: 222 us -> 213 us
    ppermute x60 -> x50, waiting for transfers between devices: 196 us -> 172 us  [swap(): return lax.ppermute(block, axis, [(i, i ^ distance) for i in range(size)])]
    ppermute x60 -> x50, starting transfers between devices: 69.2 us -> 54 us  [swap(): return lax.ppermute(block, axis, [(i, i ^ distance) for i in range(size)])]
    reduce_scatter x4, waiting for transfers between devices: 26.7 us -> 40.7 us  [home(): return lax.psum_scatter(blocks, 'row', scatter_dimension=0, tiled=True)]
    reduce_sum x16 -> x12, other arithmetic: 15.9 us -> 8.7 us  [column_dot(): return jnp.sum(first * second, axis=0)]
    pallas_call x10 -> x8, Pallas kernels: 31.2 us -> 26.3 us  [assemble(): pl.pallas_call(functools.partial(assemble_kernel, len(pieces)), out_shape...]
    unnamed x122 -> x142, local copies, waits for them, and re-layouts: 16.3 us -> 18.5 us
  transfers between devices with their start and end apart: 64 -> 54, of which waited for: 33 -> 25; matrix products, arithmetic and copies ran while one was open for 5% -> 5% of each run, Pallas kernels for 27% -> 29%
where the time goes in v1:
time: 535 us; the launch traced here: 533 us
  waiting for transfers between devices  213 us (40%)
  Pallas kernels  206 us (39%)
  starting transfers between devices  54.5 us (10%)
  other arithmetic  25.3 us (5%)
  local copies, waits for them, and re-layouts  19.8 us (4%)
  between operations  14.4 us (3%)
    ppermute x50, waiting for transfers between devices, swap(): return lax.ppermute(block, axis, [(i, i ^ distance) for i in range(size)])  172 us
    pallas_call x6, Pallas kernels, product(): pl.pallas_call(functools.partial(product_kernel, layout), out_shape=out_s...  155 us
    ppermute x50, starting transfers between devices, swap(): return lax.ppermute(block, axis, [(i, i ^ distance) for i in range(size)])  54 us
    reduce_scatter x4, waiting for transfers between devices, home(): return lax.psum_scatter(blocks, 'row', scatter_dimension=0, tiled=True)  40.7 us
    pallas_call x8, Pallas kernels, assemble(): pl.pallas_call(functools.partial(assemble_kernel, len(pieces)), out_shape...  26.3 us
    pallas_call x2, Pallas kernels, finish(): pl.pallas_call(finish_kernel, out_shape=jax.ShapeDtypeStruct(right_side.s...  20.8 us
    unnamed x142, local copies, waits for them, and re-layouts  18.5 us
  transfers between devices with their start and end apart: 54, of which 25 were waited for; matrix products, arithmetic and copies ran while one was open for 5% of the time, Pallas kernels for 29%

profile of v1, /device:TPU:0, one launch (start us, length us, event | category | flops | bytes accessed | tf_op | source)
XLA Modules:
  0.0 532.9 jit_solution(4811670448833352920)
XLA Ops:
  6.6 26.1 %shard_map.46 = (f32[576,256]{1,0:T(8,128)S(1)}, f32[576,256]{1,0:T(8,128)S(1)}, f32[576,256]{1,0:T(8,128)S(1)}, f32[576,256]{1,0:T(8,128)S(1)}) custom-call(s32[2]{0:T(128)S(1)} %pad_add_fusion.place_ref, f32[4608,2304]{1,0:T(8,128)} %h_ref.11, f32[4608,512]{1,0:T(8,128)} %right_ref.3, s32[4608,512]{1,0:T(8,128)} %mask_ref.3), custom_call_target="tpu_custom_call" | custom-call | flops 16307453952 | bytes 49545216 | tf_op jit(solution)/shard_map/pallas_call | solution.py:129
  32.7 3.0 collective-permute-start
  37.3 26.1 %shard_map.47 = (f32[576,256]{1,0:T(8,128)S(1)}, f32[576,256]{1,0:T(8,128)S(1)}, f32[576,256]{1,0:T(8,128)S(1)}, f32[576,256]{1,0:T(8,128)S(1)}) custom-call(s32[2]{0:T(128)S(1)} %pad_add_fusion.place_ref, f32[4608,2304]{1,0:T(8,128)} %h_ref.11, f32[4608,512]{1,0:T(8,128)} %right_ref.3, s32[4608,512]{1,0:T(8,128)} %mask_ref.3, ...), custom_call_target="tpu_custom_call" | custom-call | flops 16307453952 | bytes 49545216 | tf_op jit(solution)/shard_map/pallas_call | solution.py:129
  65.6 3.3 shard_map.48.refs_4_
  68.9 2.0 collective-permute-start.3
  72.5 12.7 %collective-permute-done.3.refs_1_ = f32[576,256]{1,0:T(8,128)S(1)} collective-permute-done((f32[576,256]{1,0:T(8,128)S(1)}, f32[576,256]{1,0:T(8,128)S(1)}, u32[]{:S(2)}, u32[]{:S(2)}) %collective-permute-start.3) | collective-permute-done | bytes 589856 | tf_op jit(solution)/shard_map/ppermute | solution.py:210
  85.2 12.3 %collective-permute-done.4.refs_2_ = f32[576,256]{1,0:T(8,128)S(1)} collective-permute-done((f32[576,256]{1,0:T(8,128)S(1)}, f32[576,256]{1,0:T(8,128)S(1)}, u32[]{:S(2)}, u32[]{:S(2)}) %collective-permute-start.4) | collective-permute-done | bytes 589856 | tf_op jit(solution)/shard_map/ppermute | solution.py:210
  99.2 3.4 shard_map.49
  103.5 2.0 multiply_reduce_fusion
  107.3 11.2 %reduce-scatter.5.cloned.1.call-done = f32[576,256]{1,0:T(8,128)} async-done(((f32[2304,256]{1,0:T(8,128)}), f32[576,256]{1,0:T(8,128)}) %reduce-scatter.5.cloned.1.call-update) | async-done | bytes 589840 | tf_op jit(solution)/shard_map/reduce_scatter | solution.py:286
  123.3 12.7 %collective-permute-done.6.refs_1_ = f32[576,256]{1,0:T(8,128)S(1)} collective-permute-done((f32[576,256]{1,0:T(8,128)S(1)}, f32[576,256]{1,0:T(8,128)S(1)}, u32[]{:S(2)}, u32[]{:S(2)}) %collective-permute-start.6) | collective-permute-done | bytes 589856 | tf_op jit(solution)/shard_map/ppermute | solution.py:210
  136.0 12.3 %collective-permute-done.7.refs_2_ = f32[576,256]{1,0:T(8,128)S(1)} collective-permute-done((f32[576,256]{1,0:T(8,128)S(1)}, f32[576,256]{1,0:T(8,128)S(1)}, u32[]{:S(2)}, u32[]{:S(2)}) %collective-permute-start.7) | collective-permute-done | bytes 589856 | tf_op jit(solution)/shard_map/ppermute | solution.py:210
  149.1 3.3 shard_map.50.refs_0_
  152.4 15.5 %reduce-scatter.7.cloned.1.call-done = f32[576,256]{1,0:T(8,128)} async-done(((f32[2304,256]{1,0:T(8,128)}), f32[576,256]{1,0:T(8,128)}) %reduce-scatter.7.cloned.1.call-update) | async-done | bytes 589840 | tf_op jit(solution)/shard_map/reduce_scatter | solution.py:286
  172.9 12.7 %collective-permute-done.13.refs_1_ = f32[576,256]{1,0:T(8,128)S(1)} collective-permute-done((f32[576,256]{1,0:T(8,128)S(1)}, f32[576,256]{1,0:T(8,128)S(1)}, u32[]{:S(2)}, u32[]{:S(2)}) %collective-permute-start.13) | collective-permute-done | bytes 589856 | tf_op jit(solution)/shard_map/ppermute | solution.py:210
  185.6 12.3 %collective-permute-done.14.refs_2_ = f32[576,256]{1,0:T(8,128)S(1)} collective-permute-done((f32[576,256]{1,0:T(8,128)S(1)}, f32[576,256]{1,0:T(8,128)S(1)}, u32[]{:S(2)}, u32[]{:S(2)}) %collective-permute-start.14) | collective-permute-done | bytes 589856 | tf_op jit(solution)/shard_map/ppermute | solution.py:210
  198.7 3.3 shard_map.52.refs_0_
  203.1 25.7 %shard_map.51 = (f32[576,256]{1,0:T(8,128)S(1)}, f32[576,256]{1,0:T(8,128)S(1)}, f32[576,256]{1,0:T(8,128)S(1)}, f32[576,256]{1,0:T(8,128)S(1)}, f32[4608,256]{1,0:T(8,128)}) custom-call(s32[2]{0:T(128)S(1)} %copy-done.21, f32[4608,2304]{1,0:T(8,128)} %h_ref.11, f32[2304,256]{1,0:T(8,128)S(1)} %copy-done.10, f32[2304,256]{1,0:T(8,128)} %collective-permute-done.9.refs_1_, ...), custom_call_target="tpu_custom_call" | custom-call | flops 16307453952 | bytes 49545216 | tf_op jit(solution)/shard_map/pallas_call | solution.py:129
  233.7 25.6 %shard_map.53 = (f32[576,256]{1,0:T(8,128)S(1)}, f32[576,256]{1,0:T(8,128)S(1)}, f32[576,256]{1,0:T(8,128)S(1)}, f32[576,256]{1,0:T(8,128)S(1)}, f32[4608,256]{1,0:T(8,128)}) custom-call(s32[2]{0:T(128)S(1)} %copy-done.21, f32[4608,2304]{1,0:T(8,128)} %h_ref.11, f32[2304,256]{1,0:T(8,128)S(1)} %copy-done.11, f32[2304,256]{1,0:T(8,128)} %copy-done.68, ...), custom_call_target="tpu_custom_call" | custom-call | flops 16307453952 | bytes 49545216 | tf_op jit(solution)/shard_map/pallas_call | solution.py:129
  261.3 3.3 shard_map.54
  271.5 21.2 %collective-permute-done.18 = f32[2,512]{1,0:T(2,128)S(1)} collective-permute-done((f32[2,512]{1,0:T(2,128)S(1)}, f32[2,512]{1,0:T(2,128)S(1)}, u32[]{:S(2)}, u32[]{:S(2)}) %collective-permute-start.18) | collective-permute-done | bytes 4128 | tf_op jit(solution)/shard_map/ppermute | solution.py:210
  294.2 2.2 collective-permute-done.19
  297.4 3.3 collective-permute-done.20
  302.3 4.4 collective-permute-done.21
  309.0 3.3 shard_map.56
  313.7 2.6 multiply_subtract_fusion.3
  319.8 12.7 %collective-permute-done.22.refs_1_ = f32[576,256]{1,0:T(8,128)S(1)} collective-permute-done((f32[576,256]{1,0:T(8,128)S(1)}, f32[576,256]{1,0:T(8,128)S(1)}, u32[]{:S(2)}, u32[]{:S(2)}) %collective-permute-start.22) | collective-permute-done | bytes 589856 | tf_op jit(solution)/shard_map/ppermute | solution.py:210
  332.5 10.1 %collective-permute-done.23.refs_2_ = f32[576,256]{1,0:T(8,128)S(1)} collective-permute-done((f32[576,256]{1,0:T(8,128)S(1)}, f32[576,256]{1,0:T(8,128)S(1)}, u32[]{:S(2)}, u32[]{:S(2)}) %collective-permute-start.23) | collective-permute-done | bytes 589856 | tf_op jit(solution)/shard_map/ppermute | solution.py:210
  343.5 3.3 shard_map.55.refs_0_
  346.8 14.0 %reduce-scatter.11.cloned.1.call-done = f32[576,256]{1,0:T(8,128)} async-done(((f32[2304,256]{1,0:T(8,128)}), f32[576,256]{1,0:T(8,128)}) %reduce-scatter.11.cloned.1.call-update) | async-done | bytes 589840 | tf_op jit(solution)/shard_map/reduce_scatter | solution.py:286
  362.4 2.9 multiply_reduce_fusion.2
  372.9 8.5 %collective-permute-done.38.refs_1_ = f32[576,256]{1,0:T(8,128)S(1)} collective-permute-done((f32[576,256]{1,0:T(8,128)S(1)}, f32[576,256]{1,0:T(8,128)S(1)}, u32[]{:S(2)}, u32[]{:S(2)}) %collective-permute-start.38) | collective-permute-done | bytes 589856 | tf_op jit(solution)/shard_map/ppermute | solution.py:210
  384.4 9.3 %collective-permute-done.39.refs_2_ = f32[576,256]{1,0:T(8,128)S(1)} collective-permute-done((f32[576,256]{1,0:T(8,128)S(1)}, f32[576,256]{1,0:T(8,128)S(1)}, u32[]{:S(2)}, u32[]{:S(2)}) %collective-permute-start.39) | collective-permute-done | bytes 589856 | tf_op jit(solution)/shard_map/ppermute | solution.py:210
  394.6 2.0 collective-permute-start.34
  396.6 3.3 shard_map.59.refs_0_
  403.5 2.0 collective-permute-start.31
  406.6 25.6 %shard_map.57 = (f32[576,256]{1,0:T(8,128)S(1)}, f32[576,256]{1,0:T(8,128)S(1)}, f32[576,256]{1,0:T(8,128)S(1)}, f32[576,256]{1,0:T(8,128)S(1)}, f32[4608,256]{1,0:T(8,128)}) custom-call(s32[2]{0:T(128)S(1)} %copy-done.22, f32[4608,2304]{1,0:T(8,128)} %h_ref.11, f32[2304,256]{1,0:T(8,128)S(1)} %copy-done.3, f32[2304,256]{1,0:T(8,128)} %collective-permute-done.25.refs_1_, ...), custom_call_target="tpu_custom_call" | custom-call | flops 16307453952 | bytes 49545216 | tf_op jit(solution)/shard_map/pallas_call | solution.py:129
  434.8 4.0 shard_map.58
  445.8 3.0 collective-permute-done.35
  450.4 5.6 %collective-permute-done.36 = f32[576,128]{1,0:T(8,128)S(1)} collective-permute-done((f32[576,128]{1,0:T(8,128)}, f32[576,128]{1,0:T(8,128)S(1)}, u32[]{:S(2)}, u32[]{:S(2)}) %collective-permute-start.36) | collective-permute-done | bytes 294944 | tf_op jit(solution)/shard_map/ppermute | solution.py:210
  455.9 3.4 collective-permute-start.44
  459.5 25.6 %shard_map.60 = (f32[576,256]{1,0:T(8,128)S(1)}, f32[576,256]{1,0:T(8,128)S(1)}, f32[576,256]{1,0:T(8,128)S(1)}, f32[576,256]{1,0:T(8,128)S(1)}, f32[4608,256]{1,0:T(8,128)}) custom-call(s32[2]{0:T(128)S(1)} %copy-done.22, f32[4608,2304]{1,0:T(8,128)} %h_ref.11, f32[2304,256]{1,0:T(8,128)S(1)} %copy-done.4, f32[2304,256]{1,0:T(8,128)} %collective-permute-done.41.refs_1_, ...), custom_call_target="tpu_custom_call" | custom-call | flops 16307453952 | bytes 49545216 | tf_op jit(solution)/shard_map/pallas_call | solution.py:129
  488.0 3.5 collective-permute-done.46
  492.1 3.3 collective-permute-done.47
  495.4 3.9 collective-permute-done.48
  500.2 4.0 collective-permute-done.49
  505.5 10.4 %shard_map.61.refs_0_ = f32[4608,512]{1,0:T(8,128)} custom-call(f32[3,1,256]{2,1,0:T(1,128)} %copy.6.coef_ref, f32[4608,512]{1,0:T(8,128)} %right_ref.3, s32[4608,512]{1,0:T(8,128)} %mask_ref.3, f32[4608,256]{1,0:T(8,128)} %get-tuple-element.87.u_ref, f32[4608,256]{1,0:T(8,128)} %get-tuple-element.88.r2_ref), custom_call_target="tpu_custom_call" | custom-call | flops 7077888 | bytes 23592960 | tf_op jit(solution)/shard_map/pallas_call | solution.py:250
  516.0 10.4 %shard_map.62 = f32[4608,512]{1,0:T(8,128)} custom-call(f32[3,1,256]{2,1,0:T(1,128)} %broadcast_in_dim.9.coef_ref, f32[4608,512]{1,0:T(8,128)} %right_ref.3, s32[4608,512]{1,0:T(8,128)} %mask_ref.3, f32[4608,256]{1,0:T(8,128)} %get-tuple-element.85.u_ref, f32[4608,256]{1,0:T(8,128)} %get-tuple-element.86.r2_ref, ...), custom_call_target="tpu_custom_call", output_to_operand_aliasing={{}: (5, {})} | custom-call | flops 7077888 | bytes 23592960 | tf_op jit(solution)/shard_map/pallas_call | solution.py:250
  (278 shorter events, 82.1 us)
Async XLA Ops:
  6.5 111.9 %reduce-scatter.5.cloned.1.call-start = ((), (), s32[]{:S(2)}) async-start(), calls=%async_computation.4 | async-start | bytes 2949120 | tf_op jit(solution)/shard_map/reduce_scatter | solution.py:286
  32.7 31.6 %collective-permute-start = (f32[576,256]{1,0:T(8,128)S(1)}, f32[576,256]{1,0:T(8,128)S(1)}, u32[]{:S(2)}, u32[]{:S(2)}) collective-permute-start(f32[576,256]{1,0:T(8,128)S(1)} %get-tuple-element.48), channel_id=1, source_target_pairs={{0,2},{1,3},{2,0},{3,1},{4,6},{5,7},{6,4},{7,5},{8,10},{9,11},{10,... | collective-permute-start | bytes 1769480 | tf_op jit(solution)/shard_map/ppermute | solution.py:210
  35.8 28.5 %collective-permute-start.1 = (f32[576,256]{1,0:T(8,128)S(1)}, f32[576,256]{1,0:T(8,128)S(1)}, u32[]{:S(2)}, u32[]{:S(2)}) collective-permute-start(f32[576,256]{1,0:T(8,128)S(1)} %get-tuple-element.49), channel_id=1, source_target_pairs={{0,4},{1,5},{2,6},{3,7},{4,0},{5,1},{6,2},{7,3},{8,12},{9,13},{10,... | collective-permute-start | bytes 1769480 | tf_op jit(solution)/shard_map/ppermute | solution.py:210
  37.3 27.0 %collective-permute-start.2 = (f32[576,256]{1,0:T(8,128)S(1)}, f32[576,256]{1,0:T(8,128)S(1)}, u32[]{:S(2)}, u32[]{:S(2)}) collective-permute-start(f32[576,256]{1,0:T(8,128)S(1)} %get-tuple-element.50), channel_id=1, source_target_pairs={{0,6},{1,7},{2,4},{3,5},{4,2},{5,3},{6,0},{7,1},{8,14},{9,15},{10,... | collective-permute-start | bytes 1769480 | tf_op jit(solution)/shard_map/ppermute | solution.py:210
  68.9 99.0 %reduce-scatter.7.cloned.1.call-start = ((), (), s32[]{:S(2)}) async-start(), calls=%async_computation.5 | async-start | bytes 2949120 | tf_op jit(solution)/shard_map/reduce_scatter | solution.py:286
  68.9 16.3 %collective-permute-start.3 = (f32[576,256]{1,0:T(8,128)S(1)}, f32[576,256]{1,0:T(8,128)S(1)}, u32[]{:S(2)}, u32[]{:S(2)}) collective-permute-start(f32[576,256]{1,0:T(8,128)S(1)} %get-tuple-element.52), channel_id=1, source_target_pairs={{0,2},{1,3},{2,0},{3,1},{4,6},{5,7},{6,4},{7,5},{8,10},{9,11},{10,... | collective-permute-start | bytes 1769480 | tf_op jit(solution)/shard_map/ppermute | solution.py:210
  71.0 26.6 %collective-permute-start.4 = (f32[576,256]{1,0:T(8,128)S(1)}, f32[576,256]{1,0:T(8,128)S(1)}, u32[]{:S(2)}, u32[]{:S(2)}) collective-permute-start(f32[576,256]{1,0:T(8,128)S(1)} %get-tuple-element.53), channel_id=1, source_target_pairs={{0,4},{1,5},{2,6},{3,7},{4,0},{5,1},{6,2},{7,3},{8,12},{9,13},{10,... | collective-permute-start | bytes 1769480 | tf_op jit(solution)/shard_map/ppermute | solution.py:210
  72.5 25.1 %collective-permute-start.5 = (f32[576,256]{1,0:T(8,128)S(1)}, f32[576,256]{1,0:T(8,128)S(1)}, u32[]{:S(2)}, u32[]{:S(2)}) collective-permute-start(f32[576,256]{1,0:T(8,128)S(1)} %get-tuple-element.54), channel_id=1, source_target_pairs={{0,6},{1,7},{2,4},{3,5},{4,2},{5,3},{6,0},{7,1},{8,14},{9,15},{10,... | collective-permute-start | bytes 1769480 | tf_op jit(solution)/shard_map/ppermute | solution.py:210
  102.6 210.4 %reduce-scatter.9.cloned.1.call-start = ((), (), s32[]{:S(2)}) async-start(), calls=%async_computation.6 | async-start | bytes 2949120 | tf_op jit(solution)/shard_map/reduce_scatter | solution.py:286
  119.7 16.3 %collective-permute-start.6 = (f32[576,256]{1,0:T(8,128)S(1)}, f32[576,256]{1,0:T(8,128)S(1)}, u32[]{:S(2)}, u32[]{:S(2)}) collective-permute-start(f32[576,256]{1,0:T(8,128)S(1)} %add_multiply_fusion.3.refs_0_), channel_id=1, source_target_pairs={{0,2},{1,3},{2,0},{3,1},{4,6},{5,7},{6,4},{7,5},{8,10},{9,11},{10,... | collective-permute-start | bytes 1769480 | tf_op jit(solution)/shard_map/ppermute | solution.py:210
  121.3 27.0 %collective-permute-start.7 = (f32[576,256]{1,0:T(8,128)S(1)}, f32[576,256]{1,0:T(8,128)S(1)}, u32[]{:S(2)}, u32[]{:S(2)}) collective-permute-start(f32[576,256]{1,0:T(8,128)S(1)} %add_multiply_fusion.3.refs_0_), channel_id=1, source_target_pairs={{0,4},{1,5},{2,6},{3,7},{4,0},{5,1},{6,2},{7,3},{8,12},{9,13},{10,... | collective-permute-start | bytes 1769480 | tf_op jit(solution)/shard_map/ppermute | solution.py:210
  122.7 26.4 %collective-permute-start.8 = (f32[576,256]{1,0:T(8,128)S(1)}, f32[576,256]{1,0:T(8,128)}, u32[]{:S(2)}, u32[]{:S(2)}) collective-permute-start(f32[576,256]{1,0:T(8,128)S(1)} %add_multiply_fusion.3.refs_0_), channel_id=1, source_target_pairs={{0,6},{1,7},{2,4},{3,5},{4,2},{5,3},{6,0},{7,1},{8,14},{9,15},{10,... | collective-permute-start | bytes 1769480 | tf_op jit(solution)/shard_map/ppermute | solution.py:210
  152.4 49.7 %collective-permute-start.9 = (f32[2304,256]{1,0:T(8,128)}, f32[2304,256]{1,0:T(8,128)}, u32[]{:S(2)}, u32[]{:S(2)}) collective-permute-start(f32[2304,256]{1,0:T(8,128)} %shard_map.50.refs_0_), channel_id=1, source_target_pairs={{0,1},{1,0},{2,3},{3,2},{4,5},{5,4},{6,7},{7,6},{8,9},{9,8},{10,11... | collective-permute-start | bytes 7077896 | tf_op jit(solution)/shard_map/ppermute | solution.py:210
  169.3 16.3 %collective-permute-start.13 = (f32[576,256]{1,0:T(8,128)S(1)}, f32[576,256]{1,0:T(8,128)S(1)}, u32[]{:S(2)}, u32[]{:S(2)}) collective-permute-start(f32[576,256]{1,0:T(8,128)S(1)} %add_multiply_fusion.2.refs_2_.refs_0_), channel_id=1, source_target_pairs={{0,2},{1,3},{2,0},{3,1},{4,6},{5,7},{6,4},{7,5},{8,10},{9,11},{10,... | collective-permute-start | bytes 1769480 | tf_op jit(solution)/shard_map/ppermute | solution.py:210
  170.8 27.1 %collective-permute-start.14 = (f32[576,256]{1,0:T(8,128)S(1)}, f32[576,256]{1,0:T(8,128)S(1)}, u32[]{:S(2)}, u32[]{:S(2)}) collective-permute-start(f32[576,256]{1,0:T(8,128)S(1)} %add_multiply_fusion.2.refs_2_.refs_0_), channel_id=1, source_target_pairs={{0,4},{1,5},{2,6},{3,7},{4,0},{5,1},{6,2},{7,3},{8,12},{9,13},{10,... | collective-permute-start | bytes 1769480 | tf_op jit(solution)/shard_map/ppermute | solution.py:210
  172.3 26.4 %collective-permute-start.15 = (f32[576,256]{1,0:T(8,128)S(1)}, f32[576,256]{1,0:T(8,128)}, u32[]{:S(2)}, u32[]{:S(2)}) collective-permute-start(f32[576,256]{1,0:T(8,128)S(1)} %add_multiply_fusion.2.refs_2_.refs_0_), channel_id=1, source_target_pairs={{0,6},{1,7},{2,4},{3,5},{4,2},{5,3},{6,0},{7,1},{8,14},{9,15},{10,... | collective-permute-start | bytes 1769480 | tf_op jit(solution)/shard_map/ppermute | solution.py:210
  202.1 30.3 %collective-permute-start.16 = (f32[2304,256]{1,0:T(8,128)}, f32[2304,256]{1,0:T(8,128)S(1)}, u32[]{:S(2)}, u32[]{:S(2)}) collective-permute-start(f32[2304,256]{1,0:T(8,128)} %shard_map.52.refs_0_), channel_id=1, source_target_pairs={{0,1},{1,0},{2,3},{3,2},{4,5},{5,4},{6,7},{7,6},{8,9},{9,8},{10,11... | collective-permute-start | bytes 7077896 | tf_op jit(solution)/shard_map/ppermute | solution.py:210
  228.8 31.3 %collective-permute-start.10 = (f32[576,256]{1,0:T(8,128)S(1)}, f32[576,256]{1,0:T(8,128)S(1)}, u32[]{:S(2)}, u32[]{:S(2)}) collective-permute-start(f32[576,256]{1,0:T(8,128)S(1)} %get-tuple-element.57), channel_id=1, source_target_pairs={{0,2},{1,3},{2,0},{3,1},{4,6},{5,7},{6,4},{7,5},{8,10},{9,11},{10,... | collective-permute-start | bytes 1769480 | tf_op jit(solution)/shard_map/ppermute | solution.py:210
  229.3 30.9 %collective-permute-start.11 = (f32[576,256]{1,0:T(8,128)S(1)}, f32[576,256]{1,0:T(8,128)S(1)}, u32[]{:S(2)}, u32[]{:S(2)}) collective-permute-start(f32[576,256]{1,0:T(8,128)S(1)} %get-tuple-element.58), channel_id=1, source_target_pairs={{0,4},{1,5},{2,6},{3,7},{4,0},{5,1},{6,2},{7,3},{8,12},{9,13},{10,... | collective-permute-start | bytes 1769480 | tf_op jit(solution)/shard_map/ppermute | solution.py:210
  230.8 29.3 %collective-permute-start.12 = (f32[576,256]{1,0:T(8,128)S(1)}, f32[576,256]{1,0:T(8,128)S(1)}, u32[]{:S(2)}, u32[]{:S(2)}) collective-permute-start(f32[576,256]{1,0:T(8,128)S(1)} %get-tuple-element.59), channel_id=1, source_target_pairs={{0,6},{1,7},{2,4},{3,5},{4,2},{5,3},{6,0},{7,1},{8,14},{9,15},{10,... | collective-permute-start | bytes 1769480 | tf_op jit(solution)/shard_map/ppermute | solution.py:210
  264.7 96.1 %reduce-scatter.11.cloned.1.call-start = ((), (), s32[]{:S(2)}) async-start(), calls=%async_computation.7 | async-start | bytes 2949120 | tf_op jit(solution)/shard_map/reduce_scatter | solution.py:286
  264.9 42.4 %collective-permute-start.26 = (f32[576,256]{1,0:T(8,128)S(1)}, f32[576,256]{1,0:T(8,128)S(1)}, u32[]{:S(2)}, u32[]{:S(2)}) collective-permute-start(f32[576,256]{1,0:T(8,128)S(1)} %get-tuple-element.63), channel_id=1, source_target_pairs={{0,2},{1,3},{2,0},{3,1},{4,6},{5,7},{6,4},{7,5},{8,10},{9,11},{10,... | collective-permute-start | bytes 1769480 | tf_op jit(solution)/shard_map/ppermute | solution.py:210
  265.4 41.9 %collective-permute-start.27 = (f32[576,256]{1,0:T(8,128)S(1)}, f32[576,256]{1,0:T(8,128)S(1)}, u32[]{:S(2)}, u32[]{:S(2)}) collective-permute-start(f32[576,256]{1,0:T(8,128)S(1)} %get-tuple-element.64), channel_id=1, source_target_pairs={{0,4},{1,5},{2,6},{3,7},{4,0},{5,1},{6,2},{7,3},{8,12},{9,13},{10,... | collective-permute-start | bytes 1769480 | tf_op jit(solution)/shard_map/ppermute | solution.py:210
  267.0 42.0 %collective-permute-start.28 = (f32[576,256]{1,0:T(8,128)S(1)}, f32[576,256]{1,0:T(8,128)}, u32[]{:S(2)}, u32[]{:S(2)}) collective-permute-start(f32[576,256]{1,0:T(8,128)S(1)} %get-tuple-element.65), channel_id=1, source_target_pairs={{0,6},{1,7},{2,4},{3,5},{4,2},{5,3},{6,0},{7,1},{8,14},{9,15},{10,... | collective-permute-start | bytes 1769480 | tf_op jit(solution)/shard_map/ppermute | solution.py:210
  271.0 21.6 %collective-permute-start.18 = (f32[2,512]{1,0:T(2,128)S(1)}, f32[2,512]{1,0:T(2,128)S(1)}, u32[]{:S(2)}, u32[]{:S(2)}) collective-permute-start(f32[2,512]{1,0:T(2,128)S(1)} %fusion.36), channel_id=1, source_target_pairs={{0,2},{1,3},{2,0},{3,1},{4,6},{5,7},{6,4},{7,5},{8,10},{9,11},{10,... | collective-permute-start | bytes 12296 | tf_op jit(solution)/shard_map/ppermute | solution.py:210
  296.3 4.4 collective-permute-start.20
  300.7 6.0 %collective-permute-start.21 = (f32[2,512]{1,0:T(2,128)S(1)}, f32[2,512]{1,0:T(2,128)S(1)}, u32[]{:S(2)}, u32[]{:S(2)}) collective-permute-start(f32[2,512]{1,0:T(2,128)S(1)} %add.456), channel_id=1, source_target_pairs={{0,16},{8,24},{16,0},{24,8},{1,17},{9,25},{17,1},{25,9},{2,18},{10... | collective-permute-start | bytes 12296 | tf_op jit(solution)/shard_map/ppermute | solution.py:210
  316.3 16.2 %collective-permute-start.22 = (f32[576,256]{1,0:T(8,128)S(1)}, f32[576,256]{1,0:T(8,128)S(1)}, u32[]{:S(2)}, u32[]{:S(2)}) collective-permute-start(f32[576,256]{1,0:T(8,128)S(1)} %get-tuple-element.71.refs_0_), channel_id=1, source_target_pairs={{0,2},{1,3},{2,0},{3,1},{4,6},{5,7},{6,4},{7,5},{8,10},{9,11},{10,... | collective-permute-start | bytes 1769480 | tf_op jit(solution)/shard_map/ppermute | solution.py:210
  316.4 26.2 %collective-permute-start.23 = (f32[576,256]{1,0:T(8,128)S(1)}, f32[576,256]{1,0:T(8,128)S(1)}, u32[]{:S(2)}, u32[]{:S(2)}) collective-permute-start(f32[576,256]{1,0:T(8,128)S(1)} %get-tuple-element.71.refs_0_), channel_id=1, source_target_pairs={{0,4},{1,5},{2,6},{3,7},{4,0},{5,1},{6,2},{7,3},{8,12},{9,13},{10,... | collective-permute-start | bytes 1769480 | tf_op jit(solution)/shard_map/ppermute | solution.py:210
  318.1 24.6 %collective-permute-start.24 = (f32[576,256]{1,0:T(8,128)S(1)}, f32[576,256]{1,0:T(8,128)}, u32[]{:S(2)}, u32[]{:S(2)}) collective-permute-start(f32[576,256]{1,0:T(8,128)S(1)} %get-tuple-element.71.refs_0_), channel_id=1, source_target_pairs={{0,6},{1,7},{2,4},{3,5},{4,2},{5,3},{6,0},{7,1},{8,14},{9,15},{10,... | collective-permute-start | bytes 1769480 | tf_op jit(solution)/shard_map/ppermute | solution.py:210
  346.8 56.8 %collective-permute-start.25 = (f32[2304,256]{1,0:T(8,128)}, f32[2304,256]{1,0:T(8,128)}, u32[]{:S(2)}, u32[]{:S(2)}) collective-permute-start(f32[2304,256]{1,0:T(8,128)} %shard_map.55.refs_0_), channel_id=1, source_target_pairs={{0,1},{1,0},{2,3},{3,2},{4,5},{5,4},{6,7},{7,6},{8,9},{9,8},{10,11... | collective-permute-start | bytes 7077896 | tf_op jit(solution)/shard_map/ppermute | solution.py:210
  365.2 16.2 %collective-permute-start.38 = (f32[576,256]{1,0:T(8,128)S(1)}, f32[576,256]{1,0:T(8,128)S(1)}, u32[]{:S(2)}, u32[]{:S(2)}) collective-permute-start(f32[576,256]{1,0:T(8,128)S(1)} %get-tuple-element.72.refs_2_.refs_0_), channel_id=1, source_target_pairs={{0,2},{1,3},{2,0},{3,1},{4,6},{5,7},{6,4},{7,5},{8,10},{9,11},{10,... | collective-permute-start | bytes 1769480 | tf_op jit(solution)/shard_map/ppermute | solution.py:210
  366.7 27.0 %collective-permute-start.39 = (f32[576,256]{1,0:T(8,128)S(1)}, f32[576,256]{1,0:T(8,128)S(1)}, u32[]{:S(2)}, u32[]{:S(2)}) collective-permute-start(f32[576,256]{1,0:T(8,128)S(1)} %get-tuple-element.72.refs_2_.refs_0_), channel_id=1, source_target_pairs={{0,4},{1,5},{2,6},{3,7},{4,0},{5,1},{6,2},{7,3},{8,12},{9,13},{10,... | collective-permute-start | bytes 1769480 | tf_op jit(solution)/shard_map/ppermute | solution.py:210
  368.2 28.4 %collective-permute-start.40 = (f32[576,256]{1,0:T(8,128)S(1)}, f32[576,256]{1,0:T(8,128)}, u32[]{:S(2)}, u32[]{:S(2)}) collective-permute-start(f32[576,256]{1,0:T(8,128)S(1)} %get-tuple-element.72.refs_2_.refs_0_), channel_id=1, source_target_pairs={{0,6},{1,7},{2,4},{3,5},{4,2},{5,3},{6,0},{7,1},{8,14},{9,15},{10,... | collective-permute-start | bytes 1769480 | tf_op jit(solution)/shard_map/ppermute | solution.py:210
  369.8 31.3 %collective-permute-start.32 = (f32[576,128]{1,0:T(8,128)}, f32[576,128]{1,0:T(8,128)}, u32[]{:S(2)}, u32[]{:S(2)}) collective-permute-start(f32[576,128]{1,0:T(8,128)} %get-tuple-element.166), channel_id=1, source_target_pairs={{0,8},{8,0},{16,24},{24,16},{1,9},{9,1},{17,25},{25,17},{2,10},{10... | collective-permute-start | bytes 884744 | tf_op jit(solution)/shard_map/ppermute | solution.py:210
  381.4 20.4 %collective-permute-start.33 = (f32[576,128]{1,0:T(8,128)}, f32[576,128]{1,0:T(8,128)}, u32[]{:S(2)}, u32[]{:S(2)}) collective-permute-start(f32[576,128]{1,0:T(8,128)} %get-tuple-element.165), channel_id=1, source_target_pairs={{0,16},{8,24},{16,0},{24,8},{1,17},{9,25},{17,1},{25,9},{2,18},{10... | collective-permute-start | bytes 884744 | tf_op jit(solution)/shard_map/ppermute | solution.py:210
  394.6 40.2 %collective-permute-start.34 = (f32[576,128]{1,0:T(8,128)}, f32[576,128]{1,0:T(8,128)}, u32[]{:S(2)}, u32[]{:S(2)}) collective-permute-start(f32[576,128]{1,0:T(8,128)} %get-tuple-element.164), channel_id=1, source_target_pairs={{0,24},{8,16},{16,8},{24,0},{1,25},{9,17},{17,9},{25,1},{2,26},{10... | collective-permute-start | bytes 884744 | tf_op jit(solution)/shard_map/ppermute | solution.py:210
  399.8 59.7 %collective-permute-start.41 = (f32[2304,256]{1,0:T(8,128)}, f32[2304,256]{1,0:T(8,128)}, u32[]{:S(2)}, u32[]{:S(2)}) collective-permute-start(f32[2304,256]{1,0:T(8,128)} %shard_map.59.refs_0_), channel_id=1, source_target_pairs={{0,1},{1,0},{2,3},{3,2},{4,5},{5,4},{6,7},{7,6},{8,9},{9,8},{10,11... | collective-permute-start | bytes 7077896 | tf_op jit(solution)/shard_map/ppermute | solution.py:210
  401.1 33.6 %collective-permute-start.29 = (f32[576,128]{1,0:T(8,128)}, f32[576,128]{1,0:T(8,128)}, u32[]{:S(2)}, u32[]{:S(2)}) collective-permute-start(f32[576,128]{1,0:T(8,128)} %get-tuple-element.170), channel_id=1, source_target_pairs={{0,8},{8,0},{16,24},{24,16},{1,9},{9,1},{17,25},{25,17},{2,10},{10... | collective-permute-start | bytes 884744 | tf_op jit(solution)/shard_map/ppermute | solution.py:210
  401.8 32.9 %collective-permute-start.30 = (f32[576,128]{1,0:T(8,128)}, f32[576,128]{1,0:T(8,128)}, u32[]{:S(2)}, u32[]{:S(2)}) collective-permute-start(f32[576,128]{1,0:T(8,128)} %get-tuple-element.169), channel_id=1, source_target_pairs={{0,16},{8,24},{16,0},{24,8},{1,17},{9,25},{17,1},{25,9},{2,18},{10... | collective-permute-start | bytes 884744 | tf_op jit(solution)/shard_map/ppermute | solution.py:210
  403.5 31.2 %collective-permute-start.31 = (f32[576,128]{1,0:T(8,128)}, f32[576,128]{1,0:T(8,128)}, u32[]{:S(2)}, u32[]{:S(2)}) collective-permute-start(f32[576,128]{1,0:T(8,128)} %get-tuple-element.168), channel_id=1, source_target_pairs={{0,24},{8,16},{16,8},{24,0},{1,25},{9,17},{17,9},{25,1},{2,26},{10... | collective-permute-start | bytes 884744 | tf_op jit(solution)/shard_map/ppermute | solution.py:210
  438.7 10.1 %collective-permute-start.35 = (f32[576,128]{1,0:T(8,128)}, f32[576,128]{1,0:T(8,128)S(1)}, u32[]{:S(2)}, u32[]{:S(2)}) collective-permute-start(f32[576,128]{1,0:T(8,128)} %get-tuple-element.74), channel_id=1, source_target_pairs={{0,2},{1,3},{2,0},{3,1},{4,6},{5,7},{6,4},{7,5},{8,10},{9,11},{10,... | collective-permute-start | bytes 884744 | tf_op jit(solution)/shard_map/ppermute | solution.py:210
  440.7 15.3 %collective-permute-start.36 = (f32[576,128]{1,0:T(8,128)}, f32[576,128]{1,0:T(8,128)S(1)}, u32[]{:S(2)}, u32[]{:S(2)}) collective-permute-start(f32[576,128]{1,0:T(8,128)} %get-tuple-element.75), channel_id=1, source_target_pairs={{0,4},{1,5},{2,6},{3,7},{4,0},{5,1},{6,2},{7,3},{8,12},{9,13},{10,... | collective-permute-start | bytes 884744 | tf_op jit(solution)/shard_map/ppermute | solution.py:210
  442.1 17.3 %collective-permute-start.37 = (f32[576,128]{1,0:T(8,128)}, f32[576,128]{1,0:T(8,128)S(1)}, u32[]{:S(2)}, u32[]{:S(2)}) collective-permute-start(f32[576,128]{1,0:T(8,128)} %get-tuple-element.76), channel_id=1, source_target_pairs={{0,6},{1,7},{2,4},{3,5},{4,2},{5,3},{6,0},{7,1},{8,14},{9,15},{10,... | collective-permute-start | bytes 884744 | tf_op jit(solution)/shard_map/ppermute | solution.py:210
  443.5 41.8 %collective-permute-start.42 = (f32[576,128]{1,0:T(8,128)}, f32[576,128]{1,0:T(8,128)S(1)}, u32[]{:S(2)}, u32[]{:S(2)}) collective-permute-start(f32[576,128]{1,0:T(8,128)} %get-tuple-element.82), channel_id=1, source_target_pairs={{0,2},{1,3},{2,0},{3,1},{4,6},{5,7},{6,4},{7,5},{8,10},{9,11},{10,... | collective-permute-start | bytes 884744 | tf_op jit(solution)/shard_map/ppermute | solution.py:210
  448.8 36.6 %collective-permute-start.43 = (f32[576,128]{1,0:T(8,128)S(1)}, f32[576,128]{1,0:T(8,128)S(1)}, u32[]{:S(2)}, u32[]{:S(2)}) collective-permute-start(f32[576,128]{1,0:T(8,128)S(1)} %copy-done.70), channel_id=1, source_target_pairs={{0,4},{1,5},{2,6},{3,7},{4,0},{5,1},{6,2},{7,3},{8,12},{9,13},{10,... | collective-permute-start | bytes 884744 | tf_op jit(solution)/shard_map/ppermute | solution.py:210
  455.9 30.0 %collective-permute-start.44 = (f32[576,128]{1,0:T(8,128)S(1)}, f32[576,128]{1,0:T(8,128)S(1)}, u32[]{:S(2)}, u32[]{:S(2)}) collective-permute-start(f32[576,128]{1,0:T(8,128)S(1)} %copy-done.69), channel_id=1, source_target_pairs={{0,6},{1,7},{2,4},{3,5},{4,2},{5,3},{6,0},{7,1},{8,14},{9,15},{10,... | collective-permute-start | bytes 884744 | tf_op jit(solution)/shard_map/ppermute | solution.py:210
  499.4 4.8 collective-permute-start.49
  (77 other events, 695.3 us)
Sparse Core Ops, SparseCore 0:
  69.0 49.3 reduce-scatter.4
  120.8 47.0 reduce-scatter.6
  264.8 46.6 reduce-scatter.8
  313.7 47.0 reduce-scatter.10

commit v2 on v1

--- a/solution.py
+++ b/solution.py
@@ -211,7 +211,6 @@
 
 
 def total(parts):
-    parts = jnp.stack(parts)
     for axis in ("col", "row"):
         distance = 1
         while distance < lax.axis_size(axis):
@@ -348,32 +347,44 @@
     got = [exchange(seconds[c]) for c in each]
     blocks = [place_blocks(got[0], seconds[-1][:1])]
     u_late, _ = lax.optimization_barrier((u_own, blocks[0]))
-    scalars = total(
-        [
-            column_dot(r0_all, r0_all),
-            jnp.concatenate([column_dot(r0_own[c], u_late[c]) for c in each]),
-        ]
-    )
+    over_u = jnp.concatenate([column_dot(r0_own[c], u_late[c]) for c in each])
+    scalars = total(jnp.stack([column_dot(r0_all, r0_all), over_u]))
     blocks += [place_blocks(got[c], [scalars]) for c in each[1:]]
 
     def hold(value, *others):
         return lax.optimization_barrier((value, others))[0]
 
-    kept, gathered = [], []
+    kept, gathered, dots = [], [], []
     for c in each:
         n0, c00 = scalars[:, cuts[c]]
         summed = home(blocks[c])
         if c:
-            summed = hold(summed, gathered[-1][0])
+            summed = hold(summed, gathered[-1][0], dots[-1])
         uu_own = masked(mask_own[c], summed, u_own[c])
         a0 = n0 / (c00 + epsilon)
         r1_own = r0_own[c] - a0 * u_own[c]
         s1_own = u_own[c] - a0 * uu_own
         w_own = r1_own - a0 * s1_own
         gathered.append(to_plane(w_own))
-        kept.append((a0, gathered[c][0], r1_own, s1_own, w_own, uu_own))
-    w_last = kept[-1][4]
-    got = [levels_of(hold(kept[c][4], w_last)) for c in each]
+        kept.append((a0, gathered[c][0], w_own))
+        u_c = u_own[c]
+        pairs = (
+            (r1_own, r1_own),
+            (r1_own, s1_own),
+            (r0_own[c], s1_own),
+            (r1_own, u_c),
+            (w_own, w_own),
+            (w_own, r1_own),
+            (w_own, u_c),
+            (w_own, s1_own),
+            (w_own, uu_own),
+            (u_c, uu_own),
+            (u_c, u_c),
+            (u_c, s1_own),
+        )
+        dots.append(jnp.stack([column_dot(*pair) for pair in pairs]))
+    w_last = kept[-1][2]
+    got = [levels_of(hold(kept[c][2], summed if c < 1 else w_last)) for c in each]
     others, thirds, w = [], [], []
     for c in each:
         after = [w_last]
@@ -386,17 +397,9 @@
         )
         thirds.append(pieces)
         w.append(whole)
-    rows_of = []
-    for c in each:
-        a0, mine, r1, s1, w_own, uu = kept[c]
-        u_c = u_own[c]
-        form = form_of(thirds[c], others[c], mine)
-        pairs = (
-            (r1, r1), (r1, s1), (r0_own[c], s1), (r1, u_c), (w_own, w_own), (w_own, r1),
-            (w_own, u_c), (w_own, s1), (w_own, uu), (u_c, uu), (u_c, u_c), (u_c, s1),
-        )
-        rows_of.append([form] + [column_dot(*pair) for pair in pairs])
-    sums = total([jnp.concatenate(part) for part in zip(*rows_of)])
+    forms = [form_of(thirds[c], others[c], kept[c][1])[None] for c in each]
+    rows_of = [jnp.concatenate(part) for part in zip(forms, dots)]
+    sums = total(jnp.concatenate(rows_of, axis=1))
     buffer = None
     for c in each:
         n0, c00 = scalars[:, cuts[c]]

time: 535 us -> 531 us (level)
    unnamed x142 -> x160, local copies, waits for them, and re-layouts: 18.5 us -> 18.7 us
  transfers between devices with their start and end apart: 54 -> 54, of which waited for: 25 -> 25; matrix products, arithmetic and copies ran while one was open for 5% -> 4% of each run, Pallas kernels for 29% -> 29%
where the time goes in v2:
time: 531 us; the launch traced here: 529 us
  waiting for transfers between devices  213 us (40%)
  Pallas kernels  206 us (39%)
  starting transfers between devices  55.4 us (10%)
  other arithmetic  20.9 us (4%)
  local copies, waits for them, and re-layouts  20 us (4%)
  between operations  14.7 us (3%)
    ppermute x50, waiting for transfers between devices, swap(): return lax.ppermute(block, axis, [(i, i ^ distance) for i in range(size)])  172 us
    pallas_call x6, Pallas kernels, product(): pl.pallas_call(functools.partial(product_kernel, layout), out_shape=out_s...  155 us
    ppermute x50, starting transfers between devices, swap(): return lax.ppermute(block, axis, [(i, i ^ distance) for i in range(size)])  54.9 us
    reduce_scatter x4, waiting for transfers between devices, home(): return lax.psum_scatter(blocks, 'row', scatter_dimension=0, tiled=True)  40.1 us
    pallas_call x8, Pallas kernels, assemble(): pl.pallas_call(functools.partial(assemble_kernel, len(pieces)), out_shape...  26.4 us
    pallas_call x2, Pallas kernels, finish(): pl.pallas_call(finish_kernel, out_shape=jax.ShapeDtypeStruct(right_side.s...  20.8 us
    unnamed x160, local copies, waits for them, and re-layouts  18.7 us
  transfers between devices with their start and end apart: 54, of which 25 were waited for; matrix products, arithmetic and copies ran while one was open for 4% of the time, Pallas kernels for 29%

profile of v2, /device:TPU:0, one launch (start us, length us, event | category | flops | bytes accessed | tf_op | source)
XLA Modules:
  0.0 529.4 jit_solution(10797236589034585170)
XLA Ops:
  6.6 26.1 %shard_map.46 = (f32[576,256]{1,0:T(8,128)S(1)}, f32[576,256]{1,0:T(8,128)S(1)}, f32[576,256]{1,0:T(8,128)S(1)}, f32[576,256]{1,0:T(8,128)S(1)}) custom-call(s32[2]{0:T(128)S(1)} %pad_add_fusion.place_ref, f32[4608,2304]{1,0:T(8,128)} %h_ref.11, f32[4608,512]{1,0:T(8,128)} %right_ref.3, s32[4608,512]{1,0:T(8,128)} %mask_ref.3), custom_call_target="tpu_custom_call" | custom-call | flops 16307453952 | bytes 49545216 | tf_op jit(solution)/shard_map/pallas_call | solution.py:129
  32.7 3.0 collective-permute-start
  37.3 26.1 %shard_map.47 = (f32[576,256]{1,0:T(8,128)S(1)}, f32[576,256]{1,0:T(8,128)S(1)}, f32[576,256]{1,0:T(8,128)S(1)}, f32[576,256]{1,0:T(8,128)S(1)}) custom-call(s32[2]{0:T(128)S(1)} %pad_add_fusion.place_ref, f32[4608,2304]{1,0:T(8,128)} %h_ref.11, f32[4608,512]{1,0:T(8,128)} %right_ref.3, s32[4608,512]{1,0:T(8,128)} %mask_ref.3, ...), custom_call_target="tpu_custom_call" | custom-call | flops 16307453952 | bytes 49545216 | tf_op jit(solution)/shard_map/pallas_call | solution.py:129
  65.6 3.3 shard_map.48.refs_4_
  72.5 12.7 %collective-permute-done.3.refs_1_ = f32[576,256]{1,0:T(8,128)S(1)} collective-permute-done((f32[576,256]{1,0:T(8,128)S(1)}, f32[576,256]{1,0:T(8,128)S(1)}, u32[]{:S(2)}, u32[]{:S(2)}) %collective-permute-start.3) | collective-permute-done | bytes 589856 | tf_op jit(solution)/shard_map/ppermute | solution.py:210
  85.2 12.3 %collective-permute-done.4.refs_2_ = f32[576,256]{1,0:T(8,128)S(1)} collective-permute-done((f32[576,256]{1,0:T(8,128)S(1)}, f32[576,256]{1,0:T(8,128)S(1)}, u32[]{:S(2)}, u32[]{:S(2)}) %collective-permute-start.4) | collective-permute-done | bytes 589856 | tf_op jit(solution)/shard_map/ppermute | solution.py:210
  99.2 3.4 shard_map.49
  104.8 2.4 multiply_reduce_fusion
  107.2 11.2 %reduce-scatter.5.cloned.1.call-done = f32[576,256]{1,0:T(8,128)} async-done(((f32[2304,256]{1,0:T(8,128)}), f32[576,256]{1,0:T(8,128)}) %reduce-scatter.5.cloned.1.call-update) | async-done | bytes 589840 | tf_op jit(solution)/shard_map/reduce_scatter | solution.py:285
  119.7 2.4 collective-permute-start.8
  123.3 13.7 %collective-permute-done.8.refs_3_ = f32[576,256]{1,0:T(8,128)S(1)} collective-permute-done((f32[576,256]{1,0:T(8,128)S(1)}, f32[576,256]{1,0:T(8,128)S(1)}, u32[]{:S(2)}, u32[]{:S(2)}) %collective-permute-start.8) | collective-permute-done | bytes 589856 | tf_op jit(solution)/shard_map/ppermute | solution.py:210
  136.9 11.1 %collective-permute-done.7.refs_2_ = f32[576,256]{1,0:T(8,128)S(1)} collective-permute-done((f32[576,256]{1,0:T(8,128)S(1)}, f32[576,256]{1,0:T(8,128)S(1)}, u32[]{:S(2)}, u32[]{:S(2)}) %collective-permute-start.7) | collective-permute-done | bytes 589856 | tf_op jit(solution)/shard_map/ppermute | solution.py:210
  149.6 3.3 shard_map.50.refs_0_
  153.0 14.9 %reduce-scatter.7.cloned.1.call-done = f32[576,256]{1,0:T(8,128)} async-done(((f32[2304,256]{1,0:T(8,128)}), f32[576,256]{1,0:T(8,128)}) %reduce-scatter.7.cloned.1.call-update) | async-done | bytes 589840 | tf_op jit(solution)/shard_map/reduce_scatter | solution.py:285
  169.3 2.4 collective-permute-start.15
  172.9 13.7 %collective-permute-done.15.refs_3_ = f32[576,256]{1,0:T(8,128)S(1)} collective-permute-done((f32[576,256]{1,0:T(8,128)S(1)}, f32[576,256]{1,0:T(8,128)S(1)}, u32[]{:S(2)}, u32[]{:S(2)}) %collective-permute-start.15) | collective-permute-done | bytes 589856 | tf_op jit(solution)/shard_map/ppermute | solution.py:210
  186.5 11.1 %collective-permute-done.14.refs_2_ = f32[576,256]{1,0:T(8,128)S(1)} collective-permute-done((f32[576,256]{1,0:T(8,128)S(1)}, f32[576,256]{1,0:T(8,128)S(1)}, u32[]{:S(2)}, u32[]{:S(2)}) %collective-permute-start.14) | collective-permute-done | bytes 589856 | tf_op jit(solution)/shard_map/ppermute | solution.py:210
  198.4 3.4 shard_map.52.refs_0_
  203.0 25.7 %shard_map.51 = (f32[576,256]{1,0:T(8,128)S(1)}, f32[576,256]{1,0:T(8,128)S(1)}, f32[576,256]{1,0:T(8,128)S(1)}, f32[576,256]{1,0:T(8,128)S(1)}, f32[4608,256]{1,0:T(8,128)}) custom-call(s32[2]{0:T(128)S(1)} %copy-done.21, f32[4608,2304]{1,0:T(8,128)} %h_ref.11, f32[2304,256]{1,0:T(8,128)S(1)} %copy-done.10, f32[2304,256]{1,0:T(8,128)} %collective-permute-done.9.refs_1_, ...), custom_call_target="tpu_custom_call" | custom-call | flops 16307453952 | bytes 49545216 | tf_op jit(solution)/shard_map/pallas_call | solution.py:129
  233.6 25.6 %shard_map.53 = (f32[576,256]{1,0:T(8,128)S(1)}, f32[576,256]{1,0:T(8,128)S(1)}, f32[576,256]{1,0:T(8,128)S(1)}, f32[576,256]{1,0:T(8,128)S(1)}, f32[4608,256]{1,0:T(8,128)}) custom-call(s32[2]{0:T(128)S(1)} %copy-done.21, f32[4608,2304]{1,0:T(8,128)} %h_ref.11, f32[2304,256]{1,0:T(8,128)S(1)} %copy-done.11, f32[2304,256]{1,0:T(8,128)} %copy-done.77, ...), custom_call_target="tpu_custom_call" | custom-call | flops 16307453952 | bytes 49545216 | tf_op jit(solution)/shard_map/pallas_call | solution.py:129
  261.3 3.3 shard_map.54
  272.5 20.0 %collective-permute-done.18 = f32[2,512]{1,0:T(2,128)S(1)} collective-permute-done((f32[2,512]{1,0:T(2,128)S(1)}, f32[2,512]{1,0:T(2,128)S(1)}, u32[]{:S(2)}, u32[]{:S(2)}) %collective-permute-start.18) | collective-permute-done | bytes 4128 | tf_op jit(solution)/shard_map/ppermute | solution.py:210
  294.1 2.1 collective-permute-done.19
  297.3 3.9 collective-permute-done.20
  302.2 3.9 collective-permute-done.21
  308.4 3.3 shard_map.56
  312.8 2.8 multiply_subtract_fusion.3
  319.1 13.7 %collective-permute-done.24.refs_3_ = f32[576,256]{1,0:T(8,128)S(1)} collective-permute-done((f32[576,256]{1,0:T(8,128)S(1)}, f32[576,256]{1,0:T(8,128)S(1)}, u32[]{:S(2)}, u32[]{:S(2)}) %collective-permute-start.24) | collective-permute-done | bytes 589856 | tf_op jit(solution)/shard_map/ppermute | solution.py:210
  332.8 10.2 %collective-permute-done.23.refs_2_ = f32[576,256]{1,0:T(8,128)S(1)} collective-permute-done((f32[576,256]{1,0:T(8,128)S(1)}, f32[576,256]{1,0:T(8,128)S(1)}, u32[]{:S(2)}, u32[]{:S(2)}) %collective-permute-start.23) | collective-permute-done | bytes 589856 | tf_op jit(solution)/shard_map/ppermute | solution.py:210
  343.9 3.3 shard_map.55.refs_0_
  347.2 14.0 %reduce-scatter.11.cloned.1.call-done = f32[576,256]{1,0:T(8,128)} async-done(((f32[2304,256]{1,0:T(8,128)}), f32[576,256]{1,0:T(8,128)}) %reduce-scatter.11.cloned.1.call-update) | async-done | bytes 589840 | tf_op jit(solution)/shard_map/reduce_scatter | solution.py:285
  362.6 3.3 multiply_reduce_fusion.13
  365.9 2.4 collective-permute-start.40
  372.5 10.6 %collective-permute-done.40.refs_3_ = f32[576,256]{1,0:T(8,128)S(1)} collective-permute-done((f32[576,256]{1,0:T(8,128)S(1)}, f32[576,256]{1,0:T(8,128)S(1)}, u32[]{:S(2)}, u32[]{:S(2)}) %collective-permute-start.40) | collective-permute-done | bytes 589856 | tf_op jit(solution)/shard_map/ppermute | solution.py:210
  386.0 8.2 %collective-permute-done.39.refs_2_ = f32[576,256]{1,0:T(8,128)S(1)} collective-permute-done((f32[576,256]{1,0:T(8,128)S(1)}, f32[576,256]{1,0:T(8,128)S(1)}, u32[]{:S(2)}, u32[]{:S(2)}) %collective-permute-start.39) | collective-permute-done | bytes 589856 | tf_op jit(solution)/shard_map/ppermute | solution.py:210
  396.1 2.5 collective-permute-start.34
  398.6 3.3 shard_map.59.refs_0_
  404.8 25.6 %shard_map.57 = (f32[576,256]{1,0:T(8,128)S(1)}, f32[576,256]{1,0:T(8,128)S(1)}, f32[576,256]{1,0:T(8,128)S(1)}, f32[576,256]{1,0:T(8,128)S(1)}, f32[4608,256]{1,0:T(8,128)}) custom-call(s32[2]{0:T(128)S(1)} %copy-done.22, f32[4608,2304]{1,0:T(8,128)} %h_ref.11, f32[2304,256]{1,0:T(8,128)S(1)} %copy-done.3, f32[2304,256]{1,0:T(8,128)} %collective-permute-done.25.refs_1_, ...), custom_call_target="tpu_custom_call" | custom-call | flops 16307453952 | bytes 49545216 | tf_op jit(solution)/shard_map/pallas_call | solution.py:129
  432.9 4.0 shard_map.58
  443.6 3.4 collective-permute-done.35
  448.6 5.7 %collective-permute-done.36 = f32[576,128]{1,0:T(8,128)S(1)} collective-permute-done((f32[576,128]{1,0:T(8,128)}, f32[576,128]{1,0:T(8,128)S(1)}, u32[]{:S(2)}, u32[]{:S(2)}) %collective-permute-start.36) | collective-permute-done | bytes 294944 | tf_op jit(solution)/shard_map/ppermute | solution.py:210
  455.8 25.6 %shard_map.60 = (f32[576,256]{1,0:T(8,128)S(1)}, f32[576,256]{1,0:T(8,128)S(1)}, f32[576,256]{1,0:T(8,128)S(1)}, f32[576,256]{1,0:T(8,128)S(1)}, f32[4608,256]{1,0:T(8,128)}) custom-call(s32[2]{0:T(128)S(1)} %copy-done.22, f32[4608,2304]{1,0:T(8,128)} %h_ref.11, f32[2304,256]{1,0:T(8,128)S(1)} %copy-done.4, f32[2304,256]{1,0:T(8,128)} %collective-permute-done.41.refs_1_, ...), custom_call_target="tpu_custom_call" | custom-call | flops 16307453952 | bytes 49545216 | tf_op jit(solution)/shard_map/pallas_call | solution.py:129
  485.2 2.7 collective-permute-done.46
  488.1 3.8 collective-permute-done.47
  492.1 3.7 collective-permute-done.48
  497.3 3.4 collective-permute-done.49
  502.1 10.4 %shard_map.61.refs_0_ = f32[4608,512]{1,0:T(8,128)} custom-call(f32[3,1,256]{2,1,0:T(1,128)} %copy.6.coef_ref, f32[4608,512]{1,0:T(8,128)} %right_ref.3, s32[4608,512]{1,0:T(8,128)} %mask_ref.3, f32[4608,256]{1,0:T(8,128)} %get-tuple-element.87.u_ref, f32[4608,256]{1,0:T(8,128)} %get-tuple-element.88.r2_ref), custom_call_target="tpu_custom_call" | custom-call | flops 7077888 | bytes 23592960 | tf_op jit(solution)/shard_map/pallas_call | solution.py:249
  512.4 10.4 %shard_map.62 = f32[4608,512]{1,0:T(8,128)} custom-call(f32[3,1,256]{2,1,0:T(1,128)} %broadcast_in_dim.8.coef_ref, f32[4608,512]{1,0:T(8,128)} %right_ref.3, s32[4608,512]{1,0:T(8,128)} %mask_ref.3, f32[4608,256]{1,0:T(8,128)} %get-tuple-element.85.u_ref, f32[4608,256]{1,0:T(8,128)} %get-tuple-element.86.r2_ref, ...), custom_call_target="tpu_custom_call", output_to_operand_aliasing={{}: (5, {})} | custom-call | flops 7077888 | bytes 23592960 | tf_op jit(solution)/shard_map/pallas_call | solution.py:249
  (293 shorter events, 77.5 us)
Async XLA Ops:
  6.5 111.9 %reduce-scatter.5.cloned.1.call-start = ((), (), s32[]{:S(2)}) async-start(), calls=%async_computation.4 | async-start | bytes 2949120 | tf_op jit(solution)/shard_map/reduce_scatter | solution.py:285
  32.7 31.6 %collective-permute-start = (f32[576,256]{1,0:T(8,128)S(1)}, f32[576,256]{1,0:T(8,128)S(1)}, u32[]{:S(2)}, u32[]{:S(2)}) collective-permute-start(f32[576,256]{1,0:T(8,128)S(1)} %get-tuple-element.48), channel_id=1, source_target_pairs={{0,2},{1,3},{2,0},{3,1},{4,6},{5,7},{6,4},{7,5},{8,10},{9,11},{10,... | collective-permute-start | bytes 1769480 | tf_op jit(solution)/shard_map/ppermute | solution.py:210
  35.8 28.5 %collective-permute-start.1 = (f32[576,256]{1,0:T(8,128)S(1)}, f32[576,256]{1,0:T(8,128)S(1)}, u32[]{:S(2)}, u32[]{:S(2)}) collective-permute-start(f32[576,256]{1,0:T(8,128)S(1)} %get-tuple-element.49), channel_id=1, source_target_pairs={{0,4},{1,5},{2,6},{3,7},{4,0},{5,1},{6,2},{7,3},{8,12},{9,13},{10,... | collective-permute-start | bytes 1769480 | tf_op jit(solution)/shard_map/ppermute | solution.py:210
  37.3 27.0 %collective-permute-start.2 = (f32[576,256]{1,0:T(8,128)S(1)}, f32[576,256]{1,0:T(8,128)S(1)}, u32[]{:S(2)}, u32[]{:S(2)}) collective-permute-start(f32[576,256]{1,0:T(8,128)S(1)} %get-tuple-element.50), channel_id=1, source_target_pairs={{0,6},{1,7},{2,4},{3,5},{4,2},{5,3},{6,0},{7,1},{8,14},{9,15},{10,... | collective-permute-start | bytes 1769480 | tf_op jit(solution)/shard_map/ppermute | solution.py:210
  68.9 99.0 %reduce-scatter.7.cloned.1.call-start = ((), (), s32[]{:S(2)}) async-start(), calls=%async_computation.5 | async-start | bytes 2949120 | tf_op jit(solution)/shard_map/reduce_scatter | solution.py:285
  68.9 16.3 %collective-permute-start.3 = (f32[576,256]{1,0:T(8,128)S(1)}, f32[576,256]{1,0:T(8,128)S(1)}, u32[]{:S(2)}, u32[]{:S(2)}) collective-permute-start(f32[576,256]{1,0:T(8,128)S(1)} %get-tuple-element.52), channel_id=1, source_target_pairs={{0,2},{1,3},{2,0},{3,1},{4,6},{5,7},{6,4},{7,5},{8,10},{9,11},{10,... | collective-permute-start | bytes 1769480 | tf_op jit(solution)/shard_map/ppermute | solution.py:210
  71.0 26.6 %collective-permute-start.4 = (f32[576,256]{1,0:T(8,128)S(1)}, f32[576,256]{1,0:T(8,128)S(1)}, u32[]{:S(2)}, u32[]{:S(2)}) collective-permute-start(f32[576,256]{1,0:T(8,128)S(1)} %get-tuple-element.53), channel_id=1, source_target_pairs={{0,4},{1,5},{2,6},{3,7},{4,0},{5,1},{6,2},{7,3},{8,12},{9,13},{10,... | collective-permute-start | bytes 1769480 | tf_op jit(solution)/shard_map/ppermute | solution.py:210
  72.5 25.1 %collective-permute-start.5 = (f32[576,256]{1,0:T(8,128)S(1)}, f32[576,256]{1,0:T(8,128)S(1)}, u32[]{:S(2)}, u32[]{:S(2)}) collective-permute-start(f32[576,256]{1,0:T(8,128)S(1)} %get-tuple-element.54), channel_id=1, source_target_pairs={{0,6},{1,7},{2,4},{3,5},{4,2},{5,3},{6,0},{7,1},{8,14},{9,15},{10,... | collective-permute-start | bytes 1769480 | tf_op jit(solution)/shard_map/ppermute | solution.py:210
  102.5 209.9 %reduce-scatter.9.cloned.1.call-start = ((), (), s32[]{:S(2)}) async-start(), calls=%async_computation.6 | async-start | bytes 2949120 | tf_op jit(solution)/shard_map/reduce_scatter | solution.py:285
  119.7 17.2 %collective-permute-start.8 = (f32[576,256]{1,0:T(8,128)S(1)}, f32[576,256]{1,0:T(8,128)S(1)}, u32[]{:S(2)}, u32[]{:S(2)}) collective-permute-start(f32[576,256]{1,0:T(8,128)S(1)} %add_multiply_fusion.3.refs_0_), channel_id=1, source_target_pairs={{0,6},{1,7},{2,4},{3,5},{4,2},{5,3},{6,0},{7,1},{8,14},{9,15},{10,... | collective-permute-start | bytes 1769480 | tf_op jit(solution)/shard_map/ppermute | solution.py:210
  122.2 25.8 %collective-permute-start.7 = (f32[576,256]{1,0:T(8,128)S(1)}, f32[576,256]{1,0:T(8,128)S(1)}, u32[]{:S(2)}, u32[]{:S(2)}) collective-permute-start(f32[576,256]{1,0:T(8,128)S(1)} %add_multiply_fusion.3.refs_0_), channel_id=1, source_target_pairs={{0,4},{1,5},{2,6},{3,7},{4,0},{5,1},{6,2},{7,3},{8,12},{9,13},{10,... | collective-permute-start | bytes 1769480 | tf_op jit(solution)/shard_map/ppermute | solution.py:210
  122.7 25.3 %collective-permute-start.6 = (f32[576,256]{1,0:T(8,128)S(1)}, f32[576,256]{1,0:T(8,128)S(1)}, u32[]{:S(2)}, u32[]{:S(2)}) collective-permute-start(f32[576,256]{1,0:T(8,128)S(1)} %add_multiply_fusion.3.refs_0_), channel_id=1, source_target_pairs={{0,2},{1,3},{2,0},{3,1},{4,6},{5,7},{6,4},{7,5},{8,10},{9,11},{10,... | collective-permute-start | bytes 1769480 | tf_op jit(solution)/shard_map/ppermute | solution.py:210
  152.9 49.0 %collective-permute-start.9 = (f32[2304,256]{1,0:T(8,128)}, f32[2304,256]{1,0:T(8,128)}, u32[]{:S(2)}, u32[]{:S(2)}) collective-permute-start(f32[2304,256]{1,0:T(8,128)} %shard_map.50.refs_0_), channel_id=1, source_target_pairs={{0,1},{1,0},{2,3},{3,2},{4,5},{5,4},{6,7},{7,6},{8,9},{9,8},{10,11... | collective-permute-start | bytes 7077896 | tf_op jit(solution)/shard_map/ppermute | solution.py:210
  169.3 17.2 %collective-permute-start.15 = (f32[576,256]{1,0:T(8,128)S(1)}, f32[576,256]{1,0:T(8,128)S(1)}, u32[]{:S(2)}, u32[]{:S(2)}) collective-permute-start(f32[576,256]{1,0:T(8,128)S(1)} %add_multiply_fusion.2.refs_2_.refs_0_), channel_id=1, source_target_pairs={{0,6},{1,7},{2,4},{3,5},{4,2},{5,3},{6,0},{7,1},{8,14},{9,15},{10,... | collective-permute-start | bytes 1769480 | tf_op jit(solution)/shard_map/ppermute | solution.py:210
  171.7 25.8 %collective-permute-start.14 = (f32[576,256]{1,0:T(8,128)S(1)}, f32[576,256]{1,0:T(8,128)S(1)}, u32[]{:S(2)}, u32[]{:S(2)}) collective-permute-start(f32[576,256]{1,0:T(8,128)S(1)} %add_multiply_fusion.2.refs_2_.refs_0_), channel_id=1, source_target_pairs={{0,4},{1,5},{2,6},{3,7},{4,0},{5,1},{6,2},{7,3},{8,12},{9,13},{10,... | collective-permute-start | bytes 1769480 | tf_op jit(solution)/shard_map/ppermute | solution.py:210
  172.3 26.1 %collective-permute-start.13 = (f32[576,256]{1,0:T(8,128)S(1)}, f32[576,256]{1,0:T(8,128)}, u32[]{:S(2)}, u32[]{:S(2)}) collective-permute-start(f32[576,256]{1,0:T(8,128)S(1)} %add_multiply_fusion.2.refs_2_.refs_0_), channel_id=1, source_target_pairs={{0,2},{1,3},{2,0},{3,1},{4,6},{5,7},{6,4},{7,5},{8,10},{9,11},{10,... | collective-permute-start | bytes 1769480 | tf_op jit(solution)/shard_map/ppermute | solution.py:210
  201.8 30.4 %collective-permute-start.16 = (f32[2304,256]{1,0:T(8,128)}, f32[2304,256]{1,0:T(8,128)S(1)}, u32[]{:S(2)}, u32[]{:S(2)}) collective-permute-start(f32[2304,256]{1,0:T(8,128)} %shard_map.52.refs_0_), channel_id=1, source_target_pairs={{0,1},{1,0},{2,3},{3,2},{4,5},{5,4},{6,7},{7,6},{8,9},{9,8},{10,11... | collective-permute-start | bytes 7077896 | tf_op jit(solution)/shard_map/ppermute | solution.py:210
  228.7 31.4 %collective-permute-start.10 = (f32[576,256]{1,0:T(8,128)S(1)}, f32[576,256]{1,0:T(8,128)S(1)}, u32[]{:S(2)}, u32[]{:S(2)}) collective-permute-start(f32[576,256]{1,0:T(8,128)S(1)} %get-tuple-element.57), channel_id=1, source_target_pairs={{0,2},{1,3},{2,0},{3,1},{4,6},{5,7},{6,4},{7,5},{8,10},{9,11},{10,... | collective-permute-start | bytes 1769480 | tf_op jit(solution)/shard_map/ppermute | solution.py:210
  230.1 29.9 %collective-permute-start.11 = (f32[576,256]{1,0:T(8,128)S(1)}, f32[576,256]{1,0:T(8,128)S(1)}, u32[]{:S(2)}, u32[]{:S(2)}) collective-permute-start(f32[576,256]{1,0:T(8,128)S(1)} %get-tuple-element.58), channel_id=1, source_target_pairs={{0,4},{1,5},{2,6},{3,7},{4,0},{5,1},{6,2},{7,3},{8,12},{9,13},{10,... | collective-permute-start | bytes 1769480 | tf_op jit(solution)/shard_map/ppermute | solution.py:210
  230.9 29.2 %collective-permute-start.12 = (f32[576,256]{1,0:T(8,128)S(1)}, f32[576,256]{1,0:T(8,128)S(1)}, u32[]{:S(2)}, u32[]{:S(2)}) collective-permute-start(f32[576,256]{1,0:T(8,128)S(1)} %get-tuple-element.59), channel_id=1, source_target_pairs={{0,6},{1,7},{2,4},{3,5},{4,2},{5,3},{6,0},{7,1},{8,14},{9,15},{10,... | collective-permute-start | bytes 1769480 | tf_op jit(solution)/shard_map/ppermute | solution.py:210
  264.7 96.6 %reduce-scatter.11.cloned.1.call-start = ((), (), s32[]{:S(2)}) async-start(), calls=%async_computation.7 | async-start | bytes 2949120 | tf_op jit(solution)/shard_map/reduce_scatter | solution.py:285
  264.9 41.8 %collective-permute-start.26 = (f32[576,256]{1,0:T(8,128)S(1)}, f32[576,256]{1,0:T(8,128)S(1)}, u32[]{:S(2)}, u32[]{:S(2)}) collective-permute-start(f32[576,256]{1,0:T(8,128)S(1)} %get-tuple-element.63), channel_id=1, source_target_pairs={{0,2},{1,3},{2,0},{3,1},{4,6},{5,7},{6,4},{7,5},{8,10},{9,11},{10,... | collective-permute-start | bytes 1769480 | tf_op jit(solution)/shard_map/ppermute | solution.py:210
  266.5 40.3 %collective-permute-start.27 = (f32[576,256]{1,0:T(8,128)S(1)}, f32[576,256]{1,0:T(8,128)S(1)}, u32[]{:S(2)}, u32[]{:S(2)}) collective-permute-start(f32[576,256]{1,0:T(8,128)S(1)} %get-tuple-element.64), channel_id=1, source_target_pairs={{0,4},{1,5},{2,6},{3,7},{4,0},{5,1},{6,2},{7,3},{8,12},{9,13},{10,... | collective-permute-start | bytes 1769480 | tf_op jit(solution)/shard_map/ppermute | solution.py:210
  267.2 41.2 %collective-permute-start.28 = (f32[576,256]{1,0:T(8,128)S(1)}, f32[576,256]{1,0:T(8,128)}, u32[]{:S(2)}, u32[]{:S(2)}) collective-permute-start(f32[576,256]{1,0:T(8,128)S(1)} %get-tuple-element.65), channel_id=1, source_target_pairs={{0,6},{1,7},{2,4},{3,5},{4,2},{5,3},{6,0},{7,1},{8,14},{9,15},{10,... | collective-permute-start | bytes 1769480 | tf_op jit(solution)/shard_map/ppermute | solution.py:210
  271.0 21.6 %collective-permute-start.18 = (f32[2,512]{1,0:T(2,128)S(1)}, f32[2,512]{1,0:T(2,128)S(1)}, u32[]{:S(2)}, u32[]{:S(2)}) collective-permute-start(f32[2,512]{1,0:T(2,128)S(1)} %fusion.40), channel_id=1, source_target_pairs={{0,2},{1,3},{2,0},{3,1},{4,6},{5,7},{6,4},{7,5},{8,10},{9,11},{10,... | collective-permute-start | bytes 12296 | tf_op jit(solution)/shard_map/ppermute | solution.py:210
  296.2 5.0 collective-permute-start.20
  301.2 4.9 collective-permute-start.21
  315.6 17.1 %collective-permute-start.24 = (f32[576,256]{1,0:T(8,128)S(1)}, f32[576,256]{1,0:T(8,128)S(1)}, u32[]{:S(2)}, u32[]{:S(2)}) collective-permute-start(f32[576,256]{1,0:T(8,128)S(1)} %get-tuple-element.71.refs_0_), channel_id=1, source_target_pairs={{0,6},{1,7},{2,4},{3,5},{4,2},{5,3},{6,0},{7,1},{8,14},{9,15},{10,... | collective-permute-start | bytes 1769480 | tf_op jit(solution)/shard_map/ppermute | solution.py:210
  317.2 25.8 %collective-permute-start.23 = (f32[576,256]{1,0:T(8,128)S(1)}, f32[576,256]{1,0:T(8,128)S(1)}, u32[]{:S(2)}, u32[]{:S(2)}) collective-permute-start(f32[576,256]{1,0:T(8,128)S(1)} %get-tuple-element.71.refs_0_), channel_id=1, source_target_pairs={{0,4},{1,5},{2,6},{3,7},{4,0},{5,1},{6,2},{7,3},{8,12},{9,13},{10,... | collective-permute-start | bytes 1769480 | tf_op jit(solution)/shard_map/ppermute | solution.py:210
  318.6 25.3 %collective-permute-start.22 = (f32[576,256]{1,0:T(8,128)S(1)}, f32[576,256]{1,0:T(8,128)}, u32[]{:S(2)}, u32[]{:S(2)}) collective-permute-start(f32[576,256]{1,0:T(8,128)S(1)} %get-tuple-element.71.refs_0_), channel_id=1, source_target_pairs={{0,2},{1,3},{2,0},{3,1},{4,6},{5,7},{6,4},{7,5},{8,10},{9,11},{10,... | collective-permute-start | bytes 1769480 | tf_op jit(solution)/shard_map/ppermute | solution.py:210
  347.1 56.6 %collective-permute-start.25 = (f32[2304,256]{1,0:T(8,128)}, f32[2304,256]{1,0:T(8,128)}, u32[]{:S(2)}, u32[]{:S(2)}) collective-permute-start(f32[2304,256]{1,0:T(8,128)} %shard_map.55.refs_0_), channel_id=1, source_target_pairs={{0,1},{1,0},{2,3},{3,2},{4,5},{5,4},{6,7},{7,6},{8,9},{9,8},{10,11... | collective-permute-start | bytes 7077896 | tf_op jit(solution)/shard_map/ppermute | solution.py:210
  365.9 17.1 %collective-permute-start.40 = (f32[576,256]{1,0:T(8,128)S(1)}, f32[576,256]{1,0:T(8,128)S(1)}, u32[]{:S(2)}, u32[]{:S(2)}) collective-permute-start(f32[576,256]{1,0:T(8,128)S(1)} %get-tuple-element.72.refs_2_.refs_0_), channel_id=1, source_target_pairs={{0,6},{1,7},{2,4},{3,5},{4,2},{5,3},{6,0},{7,1},{8,14},{9,15},{10,... | collective-permute-start | bytes 1769480 | tf_op jit(solution)/shard_map/ppermute | solution.py:210
  368.3 25.8 %collective-permute-start.39 = (f32[576,256]{1,0:T(8,128)S(1)}, f32[576,256]{1,0:T(8,128)S(1)}, u32[]{:S(2)}, u32[]{:S(2)}) collective-permute-start(f32[576,256]{1,0:T(8,128)S(1)} %get-tuple-element.72.refs_2_.refs_0_), channel_id=1, source_target_pairs={{0,4},{1,5},{2,6},{3,7},{4,0},{5,1},{6,2},{7,3},{8,12},{9,13},{10,... | collective-permute-start | bytes 1769480 | tf_op jit(solution)/shard_map/ppermute | solution.py:210
  368.9 26.4 %collective-permute-start.38 = (f32[576,256]{1,0:T(8,128)S(1)}, f32[576,256]{1,0:T(8,128)S(1)}, u32[]{:S(2)}, u32[]{:S(2)}) collective-permute-start(f32[576,256]{1,0:T(8,128)S(1)} %get-tuple-element.72.refs_2_.refs_0_), channel_id=1, source_target_pairs={{0,2},{1,3},{2,0},{3,1},{4,6},{5,7},{6,4},{7,5},{8,10},{9,11},{10,... | collective-permute-start | bytes 1769480 | tf_op jit(solution)/shard_map/ppermute | solution.py:210
  370.5 31.3 %collective-permute-start.31 = (f32[576,128]{1,0:T(8,128)}, f32[576,128]{1,0:T(8,128)}, u32[]{:S(2)}, u32[]{:S(2)}) collective-permute-start(f32[576,128]{1,0:T(8,128)} %get-tuple-element.168), channel_id=1, source_target_pairs={{0,24},{8,16},{16,8},{24,0},{1,25},{9,17},{17,9},{25,1},{2,26},{10... | collective-permute-start | bytes 884744 | tf_op jit(solution)/shard_map/ppermute | solution.py:210
  383.1 18.9 %collective-permute-start.30 = (f32[576,128]{1,0:T(8,128)}, f32[576,128]{1,0:T(8,128)}, u32[]{:S(2)}, u32[]{:S(2)}) collective-permute-start(f32[576,128]{1,0:T(8,128)} %get-tuple-element.169), channel_id=1, source_target_pairs={{0,16},{8,24},{16,0},{24,8},{1,17},{9,25},{17,1},{25,9},{2,18},{10... | collective-permute-start | bytes 884744 | tf_op jit(solution)/shard_map/ppermute | solution.py:210
  394.2 38.7 %collective-permute-start.29 = (f32[576,128]{1,0:T(8,128)}, f32[576,128]{1,0:T(8,128)}, u32[]{:S(2)}, u32[]{:S(2)}) collective-permute-start(f32[576,128]{1,0:T(8,128)} %get-tuple-element.170), channel_id=1, source_target_pairs={{0,8},{8,0},{16,24},{24,16},{1,9},{9,1},{17,25},{25,17},{2,10},{10... | collective-permute-start | bytes 884744 | tf_op jit(solution)/shard_map/ppermute | solution.py:210
  396.1 36.8 %collective-permute-start.34 = (f32[576,128]{1,0:T(8,128)}, f32[576,128]{1,0:T(8,128)}, u32[]{:S(2)}, u32[]{:S(2)}) collective-permute-start(f32[576,128]{1,0:T(8,128)} %get-tuple-element.164), channel_id=1, source_target_pairs={{0,24},{8,16},{16,8},{24,0},{1,25},{9,17},{17,9},{25,1},{2,26},{10... | collective-permute-start | bytes 884744 | tf_op jit(solution)/shard_map/ppermute | solution.py:210
  401.9 31.1 %collective-permute-start.33 = (f32[576,128]{1,0:T(8,128)}, f32[576,128]{1,0:T(8,128)}, u32[]{:S(2)}, u32[]{:S(2)}) collective-permute-start(f32[576,128]{1,0:T(8,128)} %get-tuple-element.165), channel_id=1, source_target_pairs={{0,16},{8,24},{16,0},{24,8},{1,17},{9,25},{17,1},{25,9},{2,18},{10... | collective-permute-start | bytes 884744 | tf_op jit(solution)/shard_map/ppermute | solution.py:210
  402.0 31.0 %collective-permute-start.32 = (f32[576,128]{1,0:T(8,128)}, f32[576,128]{1,0:T(8,128)}, u32[]{:S(2)}, u32[]{:S(2)}) collective-permute-start(f32[576,128]{1,0:T(8,128)} %get-tuple-element.166), channel_id=1, source_target_pairs={{0,8},{8,0},{16,24},{24,16},{1,9},{9,1},{17,25},{25,17},{2,10},{10... | collective-permute-start | bytes 884744 | tf_op jit(solution)/shard_map/ppermute | solution.py:210
  403.7 52.0 %collective-permute-start.41 = (f32[2304,256]{1,0:T(8,128)}, f32[2304,256]{1,0:T(8,128)}, u32[]{:S(2)}, u32[]{:S(2)}) collective-permute-start(f32[2304,256]{1,0:T(8,128)} %shard_map.59.refs_0_), channel_id=1, source_target_pairs={{0,1},{1,0},{2,3},{3,2},{4,5},{5,4},{6,7},{7,6},{8,9},{9,8},{10,11... | collective-permute-start | bytes 7077896 | tf_op jit(solution)/shard_map/ppermute | solution.py:210
  436.9 10.1 %collective-permute-start.35 = (f32[576,128]{1,0:T(8,128)}, f32[576,128]{1,0:T(8,128)S(1)}, u32[]{:S(2)}, u32[]{:S(2)}) collective-permute-start(f32[576,128]{1,0:T(8,128)} %get-tuple-element.74), channel_id=1, source_target_pairs={{0,2},{1,3},{2,0},{3,1},{4,6},{5,7},{6,4},{7,5},{8,10},{9,11},{10,... | collective-permute-start | bytes 884744 | tf_op jit(solution)/shard_map/ppermute | solution.py:210
  438.4 15.8 %collective-permute-start.36 = (f32[576,128]{1,0:T(8,128)}, f32[576,128]{1,0:T(8,128)S(1)}, u32[]{:S(2)}, u32[]{:S(2)}) collective-permute-start(f32[576,128]{1,0:T(8,128)} %get-tuple-element.75), channel_id=1, source_target_pairs={{0,4},{1,5},{2,6},{3,7},{4,0},{5,1},{6,2},{7,3},{8,12},{9,13},{10,... | collective-permute-start | bytes 884744 | tf_op jit(solution)/shard_map/ppermute | solution.py:210
  439.2 16.5 %collective-permute-start.37 = (f32[576,128]{1,0:T(8,128)}, f32[576,128]{1,0:T(8,128)S(1)}, u32[]{:S(2)}, u32[]{:S(2)}) collective-permute-start(f32[576,128]{1,0:T(8,128)} %get-tuple-element.76), channel_id=1, source_target_pairs={{0,6},{1,7},{2,4},{3,5},{4,2},{5,3},{6,0},{7,1},{8,14},{9,15},{10,... | collective-permute-start | bytes 884744 | tf_op jit(solution)/shard_map/ppermute | solution.py:210
  440.4 41.9 %collective-permute-start.42 = (f32[576,128]{1,0:T(8,128)}, f32[576,128]{1,0:T(8,128)S(1)}, u32[]{:S(2)}, u32[]{:S(2)}) collective-permute-start(f32[576,128]{1,0:T(8,128)} %get-tuple-element.82), channel_id=1, source_target_pairs={{0,2},{1,3},{2,0},{3,1},{4,6},{5,7},{6,4},{7,5},{8,10},{9,11},{10,... | collective-permute-start | bytes 884744 | tf_op jit(solution)/shard_map/ppermute | solution.py:210
  447.0 34.6 %collective-permute-start.43 = (f32[576,128]{1,0:T(8,128)S(1)}, f32[576,128]{1,0:T(8,128)S(1)}, u32[]{:S(2)}, u32[]{:S(2)}) collective-permute-start(f32[576,128]{1,0:T(8,128)S(1)} %copy-done.78), channel_id=1, source_target_pairs={{0,4},{1,5},{2,6},{3,7},{4,0},{5,1},{6,2},{7,3},{8,12},{9,13},{10,... | collective-permute-start | bytes 884744 | tf_op jit(solution)/shard_map/ppermute | solution.py:210
  454.2 27.3 %collective-permute-start.44 = (f32[576,128]{1,0:T(8,128)S(1)}, f32[576,128]{1,0:T(8,128)S(1)}, u32[]{:S(2)}, u32[]{:S(2)}) collective-permute-start(f32[576,128]{1,0:T(8,128)S(1)} %copy-done.79), channel_id=1, source_target_pairs={{0,6},{1,7},{2,4},{3,5},{4,2},{5,3},{6,0},{7,1},{8,14},{9,15},{10,... | collective-permute-start | bytes 884744 | tf_op jit(solution)/shard_map/ppermute | solution.py:210
  495.8 4.9 collective-permute-start.49
  (86 other events, 639.6 us)
Sparse Core Ops, SparseCore 0:
  69.0 49.3 reduce-scatter.4
  120.8 47.0 reduce-scatter.6
  264.8 47.1 reduce-scatter.8
  314.1 47.0 reduce-scatter.10
